TPU v7x, 256 devices: a whole 4x4x8 slice. The times are simulated.
256 devices in a mesh: space: 4 (over x_hi, core), orient: 64 (over x_lo, y, z).
Axes of the slice: x: 4 (x_hi: 2, x_lo: 2; x = x_hi * 2 + x_lo), y: 4, z: 8, core: 2. Of those that a mesh axis runs over, the one named last changes fastest.
Arguments:
- q_init: bfloat16 [256, 64, 128, 128], P('orient', 'space'), may hold values from 0.5 to 1.5
- partner: bfloat16 [256, 64, 128, 128], P('orient', 'space'), may hold values from 0.5 to 1.5
- field: bfloat16 [6, 64, 128, 128], P(None, 'space'), may hold values from -3 to 3
- orientations: float32 [3, 256], replicated, may hold values from -1 to 1, as said below
- orient_weight: float32 [256], replicated, may hold values from 0.03 to 0.12
- rotation: bfloat16 [256, 256], replicated, may hold values from -1 to 1
Outputs:
- q_final: bfloat16 [256, 64, 128, 128], P('orient', 'space')
- new_field: float32 [6, 64, 128, 128], P(None, 'space', 'orient')
Inputs may be any that keep to these rules, and one draw needn't show every extreme that they name: `orientations`: each column is a unit vector.
All inputs are finite; a program needn't handle non-finite values.
Results may differ from a plain program's by a relative error of at most 0.0057.
Values may be sent and summed in bfloat16 or wider, within the bound.
A program may use at most 128 MiB of HBM per device.

v0:
```python
import jax
import jax.numpy as jnp
from jax import lax
from jax.sharding import PartitionSpec as P

step_length = 0.3
relax_rate = 0.5
coupling = 8.0


def extended(block, sides, width):
    for axis, dim in sides:
        count = lax.axis_size(axis)
        forward = [(i, i + 1) for i in range(count - 1)]
        forward.append((count - 1, 0))
        backward = [(target, source) for source, target in forward]
        low = lax.ppermute(
            lax.slice_in_dim(block, block.shape[dim] - width, None, axis=dim), axis, forward
        )
        high = lax.ppermute(lax.slice_in_dim(block, 0, width, axis=dim), axis, backward)
        block = jnp.concatenate([low, block, high], axis=dim)
    return block


def angle_tables(orientations):
    along_x = orientations[0]
    along_y = orientations[1]
    along_z = orientations[2]
    field_terms = jnp.stack(
        [
            along_x * along_x,
            along_y * along_y,
            along_z * along_z,
            2.0 * along_x * along_y,
            2.0 * along_x * along_z,
            2.0 * along_y * along_z,
        ]
    )
    tensor_terms = jnp.stack(
        [
            along_x * along_x - 1.0 / 3.0,
            along_y * along_y - 1.0 / 3.0,
            along_z * along_z - 1.0 / 3.0,
            along_x * along_y,
            along_x * along_z,
            along_y * along_z,
        ]
    )
    return (field_terms, tensor_terms)


def upwind(center, below, above, speeds):
    speed_x, speed_y, speed_z = speeds
    back_x = center - jnp.roll(center, 1, axis=-1)
    fore_x = jnp.roll(center, -1, axis=-1) - center
    back_y = center - jnp.roll(center, 1, axis=-2)
    fore_y = jnp.roll(center, -1, axis=-2) - center
    back_z = center - below
    fore_z = above - center
    total = jnp.maximum(speed_x, 0.0) * back_x + jnp.minimum(speed_x, 0.0) * fore_x
    total = total + jnp.maximum(speed_y, 0.0) * back_y + jnp.minimum(speed_y, 0.0) * fore_y
    total = total + jnp.maximum(speed_z, 0.0) * back_z + jnp.minimum(speed_z, 0.0) * fore_z
    return center - step_length * total


def per_device(q_init, partner, field, orientations, orient_weight, rotation):
    count = q_init.shape[0]
    wide_field = field.astype(jnp.float32)
    all_terms = angle_tables(orientations)[1] * orient_weight[None, :]

    def rotate(block_in):
        flat = block_in.reshape(block_in.shape[0], -1)
        return (
            jnp.dot(rotation, flat, preferred_element_type=jnp.float32)
            .astype(jnp.bfloat16)
            .reshape(block_in.shape)
        )

    first = lax.axis_index("orient") * count
    local_dirs = lax.dynamic_slice_in_dim(orientations, first, count, 1)
    field_terms, unused_terms = angle_tables(local_dirs)
    potential = jnp.einsum(
        "co,czyx->ozyx", field_terms, wide_field, precision=lax.Precision.HIGHEST
    )
    damping = jnp.exp(-step_length * potential)
    speeds = (
        local_dirs[0][:, None, None, None],
        local_dirs[1][:, None, None, None],
        local_dirs[2][:, None, None, None],
    )

    def advance(state):
        padded = extended(state, (("space", 1),), 1).astype(jnp.float32)
        moved = upwind(padded[:, 1:-1], padded[:, :-2], padded[:, 2:], speeds)
        return (moved * damping).astype(jnp.bfloat16)

    def send_back(turned):
        return lax.all_to_all(turned, "orient", split_axis=0, concat_axis=2, tiled=True)

    def turn_back(block_in):
        return send_back(rotate(block_in))

    state = q_init
    state = turn_back(
        lax.all_to_all(advance(state), "orient", split_axis=2, concat_axis=0, tiled=True)
    )
    advected = advance(state)
    state = turn_back(lax.all_to_all(advected, "orient", split_axis=2, concat_axis=0, tiled=True))
    product = state.astype(jnp.float32) * partner.astype(jnp.float32)
    local_terms = lax.dynamic_slice_in_dim(all_terms, first, count, 1)
    partial_sum = jnp.dot(local_terms, product.reshape(count, -1), precision=lax.Precision.HIGHEST)
    partial_sum = partial_sum.reshape((6,) + product.shape[1:])
    tensor = lax.psum_scatter(partial_sum, "orient", scatter_dimension=2, tiled=True)
    owned_rows = tensor.shape[2]
    own_field = lax.dynamic_slice_in_dim(
        wide_field, lax.axis_index("orient") * owned_rows, owned_rows, 2
    )
    new_field = (1.0 - relax_rate) * own_field + relax_rate * coupling * tensor
    return (state, new_field)


def solution(mesh):
    in_specs = (
        P("orient", "space", None, None),
        P("orient", "space", None, None),
        P(None, "space", None, None),
        P(),
        P(),
        P(),
    )
    out_specs = (P("orient", "space", None, None), P(None, "space", "orient", None))
    return jax.shard_map(
        per_device, mesh=mesh, in_specs=in_specs, out_specs=out_specs, check_vma=False
    )
```

profile of v0, /device:TPU:2, one launch (start us, length us, event | category | flops | bytes accessed | tf_op | source)
XLA Modules:
  0.0 721.1 jit_solution(15064331702838822168)
XLA Ops:
  7.2 1.8 fusion.46
  9.0 3.2 collective-permute-start.1
  12.2 0.8 constant_dynamic-slice_fusion.1
  13.0 0.1 copy.153
  13.1 0.7 copy.154
  13.7 0.7 copy.155
  14.4 2.0 maximum_reduce_fusion.2
  16.4 0.8 stack.4
  17.2 6.0 fusion.31
  23.3 0.4 maximum_convert_fusion
  23.6 4.1 fusion.42
  27.8 5.0 fusion.43
  32.9 4.9 fusion.44
  37.9 13.5 %fusion.13 = bf16[4,16,128,128]{3,2,1,0:T(8,128)(2,1)} fusion(f32[4,18,128,128]{3,2,1,0:T(8,128)S(1)} %maximum_convert_fusion, f32[4,16,128,127]{3,2,1,0:T(8,128)} %get-tuple-element.29, f32[4,16,128,1]{3,2,1,0:T(8,128)} %get-tuple-element.31, f32[4,16,128,1]{3,2,1,0:T(8,128)} %get-tuple-element.30, f32[4,16,128,127]{3,2,1,0:T(8,128)} %get-tuple-element.28, ...), kind=kLoop, calls=%fused_computation.19 | loop fusion | flops 27262976 | bytes 35651680 | tf_op jit(solution)/shard_map/convert_element_type | solution.py:95
  51.4 3.2 copy.133
  54.6 63.6 %all_to_all.66 = bf16[4,16,128,128]{3,0,1,2:T(4,128)(2,1)S(1)} all-to-all(bf16[4,16,128,128]{3,0,1,2:T(4,128)(2,1)S(1)} %copy.133), channel_id=1, replica_groups=mesh['space'=4,'orient'=64] {'orient'}, dimensions={2} | all-to-all | bytes 4194304 | tf_op jit(solution)/shard_map/all_to_all | solution.py:105
  118.2 3.5 copy.174
  121.7 4.5 reshape.78
  126.2 3.7 convolution_convert_fusion.1
  129.9 4.6 copy.135
  134.5 56.4 %all_to_all.67 = bf16[256,16,2,128]{3,1,2,0:T(8,128)(2,1)S(1)} all-to-all(bf16[256,16,2,128]{3,1,2,0:T(8,128)(2,1)} %copy.135), channel_id=1, replica_groups=mesh['space'=4,'orient'=64] {'orient'}, dimensions={0} | all-to-all | bytes 4194304 | tf_op jit(solution)/shard_map/all_to_all | solution.py:98
  190.8 2.3 copy.136
  193.1 0.1 collective-permute-start.2
  193.2 3.6 collective-permute-start.3
  196.8 3.4 collective-permute-done.2
  200.3 0.4 maximum_convert_fusion.1
  200.6 4.1 fusion.39
  204.8 5.0 fusion.40
  209.8 4.9 fusion.41
  214.8 13.5 %fusion.5 = bf16[4,16,128,128]{3,2,1,0:T(8,128)(2,1)} fusion(f32[4,18,128,128]{3,2,1,0:T(8,128)S(1)} %maximum_convert_fusion.1, f32[4,16,128,127]{3,2,1,0:T(8,128)} %get-tuple-element.23, f32[4,16,128,1]{3,2,1,0:T(8,128)} %get-tuple-element.25, f32[4,16,128,1]{3,2,1,0:T(8,128)} %get-tuple-element.24, f32[4,16,128,127]{3,2,1,0:T(8,128)} %get-tuple-element.22, ...), kind=kLoop, calls=%fused_computation.9 | loop fusion | flops 27262976 | bytes 35651680 | tf_op jit(solution)/shard_map/convert_element_type | solution.py:95
  228.3 3.2 copy.137
  231.5 57.3 %all_to_all.68 = bf16[4,16,128,128]{3,0,1,2:T(4,128)(2,1)S(1)} all-to-all(bf16[4,16,128,128]{3,0,1,2:T(4,128)(2,1)S(1)} %copy.137), channel_id=1, replica_groups=mesh['space'=4,'orient'=64] {'orient'}, dimensions={2} | all-to-all | bytes 4194304 | tf_op jit(solution)/shard_map/all_to_all | solution.py:108
  288.8 3.5 copy.173
  292.3 4.5 reshape.80
  296.7 3.7 convolution_convert_fusion
  300.4 4.6 copy.139
  305.0 6.6 all-to-all-start.3
  311.8 50.8 %all-to-all-done.3 = bf16[256,16,2,128]{3,1,2,0:T(8,128)(2,1)} async-done(((bf16[256,16,2,128]{3,1,2,0:T(8,128)(2,1)}), bf16[256,16,2,128]{3,1,2,0:T(8,128)(2,1)}, u32[]{:S(2)}, u32[]{:S(2)}) %all-to-all-start.3) | async-done | bytes 2097184 | tf_op jit(solution)/shard_map/all_to_all | solution.py:98
  362.6 2.1 copy.140
  364.8 1.4 convert_multiply_fusion
  366.2 1.3 copy.143
  367.5 8.9 %copy.172 = f32[1,4,2048,128]{3,1,2,0:T(4,128)S(1)} copy(f32[1,4,2048,128]{3,2,1,0:T(8,128)S(1)} %bitcast.49) | data formatting | bytes 8388608
  376.4 7.4 %fusion.34 = f32[6,16,128,128]{3,0,2,1:T(8,128)S(1)} fusion(f32[16,128,128,4]{2,3,1,0:T(4,128)S(1)} %bitcast.48, f32[6,256]{1,0:T(8,128)S(1)} %stack.5, s32[]{:T(128)S(6)} %select_n.7, f32[4]{0:T(128)S(1)} %dynamic-slice), kind=kOutput, calls=%fused_computation.61 | convolution fusion | flops 75497496 | bytes 10490372 | tf_op jit(solution)/shard_map/dot_general | solution.py:111
  383.9 6.3 copy.146
  390.2 3.5 copy.147
  393.7 318.6 %reduce-scatter.2.cloned.1.call-done = f32[6,16,2,128]{3,1,0,2:T(8,128)} async-done(((f32[6,16,128,128]{3,1,0,2:T(8,128)}), f32[6,16,2,128]{3,1,0,2:T(8,128)}) %reduce-scatter.2.cloned.1.call-update) | async-done | bytes 98320 | tf_op jit(solution)/shard_map/reduce_scatter | solution.py:113
  712.2 0.9 multiply_add_fusion
  713.2 0.7 copy.148
  (40 shorter events, 0.5 us)
Async XLA Ops:
  7.2 10.1 %copy-start = (bf16[6,16,128,128]{3,2,1,0:T(8,128)(2,1)S(1)}, bf16[6,16,128,128]{3,2,1,0:T(8,128)(2,1)}, u32[]{:S(2)}) copy-start(bf16[6,16,128,128]{3,2,1,0:T(8,128)(2,1)} %param.8) | copy-start | bytes 9437188
  9.0 14.3 %collective-permute-start = (bf16[4,1,128,128]{3,2,1,0:T(8,128)(2,1)}, bf16[4,1,128,128]{3,2,1,0:T(8,128)(2,1)S(1)}, u32[]{:S(2)}, u32[]{:S(2)}) collective-permute-start(bf16[4,1,128,128]{3,2,1,0:T(8,128)(2,1)} %get-tuple-element.38), channel_id=1, source_target_pairs={{0,64},{64,128},{128,192},{192,0},{1,65},{65,129},{129,193},{193,1... | collective-permute-start | bytes 393224 | tf_op jit(solution)/shard_map/ppermute | solution.py:17
  9.0 14.3 %collective-permute-start.1 = (bf16[4,1,128,128]{3,2,1,0:T(8,128)(2,1)S(1)}, bf16[4,1,128,128]{3,2,1,0:T(8,128)(2,1)S(1)}, u32[]{:S(2)}, u32[]{:S(2)}) collective-permute-start(bf16[4,1,128,128]{3,2,1,0:T(8,128)(2,1)S(1)} %get-tuple-element.39), channel_id=1, source_target_pairs={{64,0},{128,64},{192,128},{0,192},{65,1},{129,65},{193,129},{1,193... | collective-permute-start | bytes 393224 | tf_op jit(solution)/shard_map/ppermute | solution.py:20
  17.2 6.0 copy-start.2
  32.8 5.0 copy-start.6
  32.8 5.0 copy-start.7
  32.8 5.0 copy-start.8
  32.8 5.1 copy-start.9
  32.8 5.1 copy-start.10
  32.8 5.1 copy-start.11
  118.2 8.0 %copy-start.4 = (bf16[256,256]{1,0:T(8,128)(2,1)S(1)}, bf16[256,256]{1,0:T(8,128)(2,1)}, u32[]{:S(2)}) copy-start(bf16[256,256]{1,0:T(8,128)(2,1)} %param.11) | copy-start | bytes 393220
  193.1 7.1 collective-permute-start.2
  193.2 7.0 collective-permute-start.3
  300.4 11.2 %copy-start.12 = (f32[256]{0:T(256)S(1)}, f32[256]{0:T(256)}, u32[]{:S(2)}) copy-start(f32[256]{0:T(256)} %param.10) | copy-start | bytes 3076
  300.4 11.3 %copy-start.5 = (f32[3,256]{1,0:T(4,128)S(1)}, f32[3,256]{1,0:T(4,128)}, u32[]{:S(2)}) copy-start(f32[3,256]{1,0:T(4,128)} %param.9) | copy-start | bytes 9220
  305.0 57.6 %all-to-all-start.3 = ((bf16[256,16,2,128]{3,1,2,0:T(8,128)(2,1)}), bf16[256,16,2,128]{3,1,2,0:T(8,128)(2,1)}, u32[]{:S(2)}, u32[]{:S(2)}) async-start(bf16[256,16,2,128]{3,1,2,0:T(8,128)(2,1)} %copy.139), calls=%async_computation.3 | async-start | bytes 4194304 | tf_op jit(solution)/shard_map/all_to_all | solution.py:98
  311.6 400.6 %reduce-scatter.2.cloned.1.call-start = ((), (), s32[]{:S(2)}) async-start(), calls=%async_computation.5 | async-start | bytes 6389760 | tf_op jit(solution)/shard_map/reduce_scatter | solution.py:113
  362.6 2.2 copy-start.3
  364.8 1.4 copy-start.1
Sparse Core Ops, SparseCore 0:
  390.3 321.9 reduce-scatter.1
where the time goes:
time: 732 us; the launch traced here: 721 us
  waiting for transfers between devices  373 us (51%)
  blocking collectives  177 us (24%)
  local copies, waits for them, and re-layouts  89.9 us (12%)
  other arithmetic  32.1 us (4%)
  matrix products  20.8 us (3%)
  between operations  14.6 us (2%)
  starting transfers between devices  13.6 us (2%)
    reduce_scatter x1, waiting for transfers between devices, per_device(): lax.psum_scatter(partial_sum, 'orient', scatter_dimension=2, tiled=True)  319 us
    all_to_all x1, blocking collectives, per_device(): lax.all_to_all(advance(state), 'orient', split_axis=2, concat_axis=0, til...  63.6 us
    all_to_all x1, blocking collectives, per_device(): lax.all_to_all(advected, 'orient', split_axis=2, concat_axis=0, tiled=True)  57.3 us
    all_to_all x1, blocking collectives, send_back(): lax.all_to_all(turned, 'orient', split_axis=0, concat_axis=2, tiled=True)  56.4 us
    all_to_all x1, waiting for transfers between devices, send_back(): lax.all_to_all(turned, 'orient', split_axis=0, concat_axis=2, tiled=True)  50.8 us
    convert_element_type x2, other arithmetic, advance(): return (moved * damping).astype(jnp.bfloat16)  27 us
    slice x4, local copies, waits for them, and re-layouts, upwind(): fore_x = jnp.roll(center, -1, axis=-1) - center  20 us
  transfers between devices with their start and end apart: 6, of which 3 were waited for; matrix products, arithmetic and copies ran while one was open for 2% of the time, Pallas kernels for 0%

commit v1 on v0

v1 whole, which is shorter than its diff:
```python
import functools

import jax
import jax.numpy as jnp
from jax import lax
from jax.experimental import pallas as pl
from jax.experimental.pallas import tpu as pltpu
from jax.sharding import PartitionSpec as P

step_length = 0.3
relax_rate = 0.5
coupling = 8.0

ZT = 2
YT = 16


def angle_tables(orientations):
    ux, uy, uz = orientations[0], orientations[1], orientations[2]
    field_terms = jnp.stack(
        [ux * ux, uy * uy, uz * uz, 2.0 * ux * uy, 2.0 * ux * uz, 2.0 * uy * uz]
    )
    third = 1.0 / 3.0
    tensor_terms = jnp.stack(
        [ux * ux - third, uy * uy - third, uz * uz - third, ux * uy, ux * uz, uy * uz]
    )
    return field_terms, tensor_terms


def split3(values):
    high = lax.reduce_precision(values, 8, 7)
    rest = values - high
    mid = lax.reduce_precision(rest, 8, 7)
    low = rest - mid
    return [piece.astype(jnp.bfloat16) for piece in (high, mid, low)]


def advect_kernel(zt, yt, coef_ref, q_ref, lo_ref, hi_ref, hlo_ref, hhi_ref, w_ref, out_ref):
    step = pl.program_id(0)
    last = pl.num_programs(0) - 1
    count = q_ref.shape[0]
    ny = q_ref.shape[2]
    nx = q_ref.shape[3]
    for zz in range(zt):
        planes = [w_ref[c, zz].astype(jnp.float32) for c in range(6)]
        for o in range(count):
            f = q_ref[o, zz].astype(jnp.float32)
            if zz > 0:
                below = q_ref[o, zz - 1].astype(jnp.float32)
            else:
                below = jnp.where(step == 0, hlo_ref[o, 0], lo_ref[o, 0]).astype(jnp.float32)
            if zz < zt - 1:
                above = q_ref[o, zz + 1].astype(jnp.float32)
            else:
                above = jnp.where(step == last, hhi_ref[o, 0], hi_ref[o, 0]).astype(jnp.float32)
            positive = [coef_ref[o, 10 + a] > 0.0 for a in range(3)]
            up_x = pltpu.roll(f, jnp.where(positive[0], 1, nx - 1), 1)
            up_y = jnp.where(positive[1], pltpu.roll(f, 1, 0), pltpu.roll(f, ny - 1, 0))
            up_z = jnp.where(positive[2], below, above)
            moved = f * coef_ref[o, 9]
            moved = moved + coef_ref[o, 6] * up_x
            moved = moved + coef_ref[o, 7] * up_y
            moved = moved + coef_ref[o, 8] * up_z
            power = coef_ref[o, 0] * planes[0]
            for c in range(1, 6):
                power = power + coef_ref[o, c] * planes[c]
            res = (moved * jnp.exp(power)).astype(jnp.bfloat16)
            for yb in range(ny // yt):
                out_ref[yb, 0, o, zz] = res[yb * yt : (yb + 1) * yt]


def rotate_kernel(yt, rot_ref, in_ref, out_ref, wide):
    no = in_ref.shape[0]
    nx = in_ref.shape[3]
    wide[...] = in_ref[:, 0].astype(jnp.float32).reshape(no * yt, nx)

    def body(y, carry):
        tile = wide[pl.ds(y, no, stride=yt), :].astype(jnp.bfloat16)
        turned = jnp.dot(rot_ref[...], tile, preferred_element_type=jnp.float32)
        out_ref[0, y] = turned.astype(jnp.bfloat16)
        return carry

    lax.fori_loop(0, yt, body, 0)


def second_kernel(
    zt,
    yt,
    rot_ref,
    coef_ref,
    ft_ref,
    tt_ref,
    q_ref,
    zlo_ref,
    zhi_ref,
    ylo_ref,
    yhi_ref,
    w_ref,
    part_ref,
    out_ref,
    field_ref,
    ext,
    wide,
    pwide,
):
    z = pl.program_id(0)
    no = q_ref.shape[2]
    nx = q_ref.shape[3]

    @pl.when(z == 0)
    def fill():
        for zz in range(zt):
            ext[zz + 1, 0] = ylo_ref[zz]
            ext[zz + 1, yt + 1] = yhi_ref[zz]
            for y in range(yt):
                ext[zz + 1, y + 1] = q_ref[zz, y]
        for y in range(yt):
            ext[0, y + 1] = zlo_ref[y]
            ext[zt + 1, y + 1] = zhi_ref[y]

    pwide[...] = part_ref[:, 0].astype(jnp.float32).reshape(no * yt, nx)

    def body(y, carry):
        f = ext[z + 1, y + 1].astype(jnp.float32)
        up_x = jnp.where(coef_ref[4] > 0, pltpu.roll(f, 1, 1), pltpu.roll(f, nx - 1, 1))
        up_y = jnp.where(
            coef_ref[5] > 0,
            ext[z + 1, y].astype(jnp.float32),
            ext[z + 1, y + 2].astype(jnp.float32),
        )
        up_z = jnp.where(
            coef_ref[6] > 0,
            ext[z, y + 1].astype(jnp.float32),
            ext[z + 2, y + 1].astype(jnp.float32),
        )
        moved = f * coef_ref[0] + coef_ref[1] * up_x + coef_ref[2] * up_y + coef_ref[3] * up_z
        w = w_ref[0, y]
        power = jnp.dot(ft_ref[...], w, preferred_element_type=jnp.float32)
        adv = (moved * jnp.exp(power)).astype(jnp.bfloat16)
        turned = jnp.dot(rot_ref[...], adv, preferred_element_type=jnp.float32)
        q2 = turned.astype(jnp.bfloat16).astype(jnp.float32)
        wide[pl.ds(y, no, stride=yt), :] = q2
        prod = q2 * pwide[pl.ds(y, no, stride=yt), :]
        high = prod.astype(jnp.bfloat16)
        low = (prod - high.astype(jnp.float32)).astype(jnp.bfloat16)
        sums = jnp.dot(tt_ref[...], high, preferred_element_type=jnp.float32)
        sums = sums + jnp.dot(tt_ref[...], low, preferred_element_type=jnp.float32)
        total = sums[0:8] + sums[8:16] + sums[16:24]
        old = w[0:8].astype(jnp.float32)
        field_ref[0, y] = (1.0 - relax_rate) * old + relax_rate * coupling * total
        return carry

    lax.fori_loop(0, yt, body, 0)
    out_ref[:, 0] = wide[...].astype(jnp.bfloat16).reshape(no, yt, nx)


def per_device(q_init, partner, field, orientations, orient_weight, rotation):
    count, nz, ny, nx = q_init.shape
    no = orientations.shape[1]
    zt, yt = ZT, YT
    nzb, nyb = nz // zt, ny // yt
    groups = nzb * nyb
    spaces = lax.axis_size("space")
    bf16 = jnp.bfloat16

    me = lax.axis_index("orient")
    my_yb = me // nzb
    my_zb = me % nzb

    field_terms, tensor_terms = angle_tables(orientations)
    magnitude = step_length * jnp.abs(orientations)
    rest = 1.0 - (magnitude[0] + magnitude[1] + magnitude[2])
    sign = jnp.where(orientations > 0.0, 1.0, 0.0)
    scaled = -step_length * field_terms

    packed = jnp.concatenate([scaled, magnitude, rest[None], sign, jnp.zeros((3, no))], axis=0)
    local = lax.dynamic_slice_in_dim(packed, me * count, count, 1).T

    forward = [(i, (i + 1) % spaces) for i in range(spaces)]
    backward = [(b, a) for a, b in forward]
    halo_lo = lax.ppermute(q_init[:, -1:], "space", forward)
    halo_hi = lax.ppermute(q_init[:, :1], "space", backward)

    plane = (count, 1, ny, nx)
    advected = pl.pallas_call(
        functools.partial(advect_kernel, zt, yt),
        grid=(nzb,),
        in_specs=[
            pl.BlockSpec(memory_space=pltpu.SMEM),
            pl.BlockSpec((count, zt, ny, nx), lambda i: (0, i, 0, 0)),
            pl.BlockSpec(plane, lambda i: (0, jnp.maximum(i * zt - 1, 0), 0, 0)),
            pl.BlockSpec(plane, lambda i: (0, jnp.minimum(i * zt + zt, nz - 1), 0, 0)),
            pl.BlockSpec(plane, lambda i: (0, 0, 0, 0)),
            pl.BlockSpec(plane, lambda i: (0, 0, 0, 0)),
            pl.BlockSpec((6, zt, ny, nx), lambda i: (0, i, 0, 0)),
        ],
        out_specs=pl.BlockSpec((nyb, 1, count, zt, yt, nx), lambda i: (0, i, 0, 0, 0, 0)),
        out_shape=jax.ShapeDtypeStruct((nyb, nzb, count, zt, yt, nx), bf16),
        compiler_params=pltpu.CompilerParams(vmem_limit_bytes=32 << 20),
        name="advect",
    )(local, q_init, q_init, q_init, halo_lo, halo_hi, field)

    def exchange(blocks):
        return lax.all_to_all(blocks, "orient", split_axis=0, concat_axis=0, tiled=True)

    part = partner.reshape(count, nzb, zt, nyb, yt, nx).transpose(3, 1, 0, 2, 4, 5)
    part = exchange(part.reshape(groups, count, zt, yt, nx)).reshape(no, zt, yt, nx)
    got = exchange(advected.reshape(groups, count, zt, yt, nx)).reshape(no, zt, yt, nx)

    state = pl.pallas_call(
        functools.partial(rotate_kernel, yt),
        grid=(zt,),
        in_specs=[
            pl.BlockSpec((no, no), lambda i: (0, 0)),
            pl.BlockSpec((no, 1, yt, nx), lambda i: (0, i, 0, 0)),
        ],
        out_specs=pl.BlockSpec((1, yt, no, nx), lambda i: (i, 0, 0, 0)),
        out_shape=jax.ShapeDtypeStruct((zt, yt, no, nx), bf16),
        scratch_shapes=[pltpu.VMEM((no * yt, nx), jnp.float32)],
        compiler_params=pltpu.CompilerParams(vmem_limit_bytes=32 << 20),
        name="rotate",
    )(rotation, got)

    z_next = []
    y_next = []
    for s in range(spaces):
        for yb in range(nyb):
            for zb in range(nzb):
                src = s * groups + yb * nzb + zb
                if zb < nzb - 1:
                    dst = src + 1
                else:
                    dst = ((s + 1) % spaces) * groups + yb * nzb
                z_next.append((src, dst))
                y_next.append((src, s * groups + ((yb + 1) % nyb) * nzb + zb))
    z_prev = [(b, a) for a, b in z_next]
    y_prev = [(b, a) for a, b in y_next]
    both = ("space", "orient")
    zlo = lax.ppermute(state[zt - 1], both, z_next)
    zhi = lax.ppermute(state[0], both, z_prev)
    ylo = lax.ppermute(state[:, yt - 1], both, y_next)
    yhi = lax.ppermute(state[:, 0], both, y_prev)

    own = lax.dynamic_slice(field, (0, my_zb * zt, my_yb * yt, 0), (6, zt, yt, nx))
    own = jnp.pad(own.transpose(1, 2, 0, 3), ((0, 0), (0, 0), (0, 2), (0, 0)))
    own3 = jnp.concatenate([own, own, own], axis=2)
    ft = jnp.pad(scaled.T, ((0, 0), (0, 2)))
    ft3 = jnp.concatenate(split3(ft), axis=1)
    tt = jnp.pad(tensor_terms * orient_weight[None, :], ((0, 2), (0, 0)))
    tt3 = jnp.concatenate(split3(tt), axis=0)
    wide_coef = jnp.concatenate([rest[None], magnitude, sign], axis=0)
    wide_coef = jnp.broadcast_to(wide_coef[:, :, None], (7, no, nx))

    full = lambda *shape: pl.BlockSpec(shape, lambda i: (0,) * len(shape))
    back, new_block = pl.pallas_call(
        functools.partial(second_kernel, zt, yt),
        grid=(zt,),
        in_specs=[
            full(no, no),
            full(7, no, nx),
            full(no, 24),
            full(24, no),
            full(zt, yt, no, nx),
            full(yt, no, nx),
            full(yt, no, nx),
            full(zt, no, nx),
            full(zt, no, nx),
            pl.BlockSpec((1, yt, 24, nx), lambda i: (i, 0, 0, 0)),
            pl.BlockSpec((no, 1, yt, nx), lambda i: (0, i, 0, 0)),
        ],
        out_specs=[
            pl.BlockSpec((no, 1, yt, nx), lambda i: (0, i, 0, 0)),
            pl.BlockSpec((1, yt, 8, nx), lambda i: (i, 0, 0, 0)),
        ],
        out_shape=[
            jax.ShapeDtypeStruct((no, zt, yt, nx), bf16),
            jax.ShapeDtypeStruct((zt, yt, 8, nx), jnp.float32),
        ],
        scratch_shapes=[
            pltpu.VMEM((zt + 2, yt + 2, no, nx), bf16),
            pltpu.VMEM((no * yt, nx), jnp.float32),
            pltpu.VMEM((no * yt, nx), jnp.float32),
        ],
        compiler_params=pltpu.CompilerParams(vmem_limit_bytes=48 << 20),
        name="second",
    )(rotation, wide_coef, ft3, tt3, state, zlo, zhi, ylo, yhi, own3, part)

    final = exchange(back.reshape(groups, count, zt, yt, nx))
    final = final.reshape(nyb, nzb, count, zt, yt, nx).transpose(2, 1, 3, 0, 4, 5)
    final = final.reshape(count, nz, ny, nx)

    pairs = ny // groups
    each = yt // pairs
    rows = new_block[:, :, :6].reshape(zt, each, pairs, 6, nx).transpose(1, 3, 0, 2, 4)
    clusters = [[g * nzb + j for j in range(nzb)] for g in range(nyb)]
    rows = lax.all_to_all(
        rows, "orient", split_axis=0, concat_axis=0, axis_index_groups=clusters, tiled=True
    )
    rows = rows.transpose(1, 0, 2, 3, 4).reshape(6, nz, pairs, nx)
    return final, rows


def solution(mesh):
    in_specs = (
        P("orient", "space", None, None),
        P("orient", "space", None, None),
        P(None, "space", None, None),
        P(),
        P(),
        P(),
    )
    out_specs = (P("orient", "space", None, None), P(None, "space", "orient", None))
    return jax.shard_map(
        per_device, mesh=mesh, in_specs=in_specs, out_specs=out_specs, check_vma=False
    )
```

time: 732 us -> 254 us (0.35); the launches traced: 721 us -> 253 us
  waiting for transfers between devices: 373 us -> 150 us
  blocking collectives: 177 us -> 11.5 us
  local copies, waits for them, and re-layouts: 89.9 us -> 17.6 us
  Pallas kernels: 0 us -> 36.1 us
  other arithmetic: 32.1 us -> 2.85 us
  matrix products: 20.8 us -> 0 us
  starting transfers between devices: 13.6 us -> 34.1 us
  between operations: 14.6 us -> 0.84 us
    reduce_scatter x1 -> x0, waiting for transfers between devices: 319 us -> none  [per_device(): lax.psum_scatter(partial_sum, 'orient', scatter_dimension=2, tiled=True)]
    all_to_all x3 -> x1, blocking collectives: 177 us -> 11.5 us  [per_device(): lax.all_to_all(rows, 'orient', split_axis=0, concat_axis=0, axis_index_gr...]
    all_to_all x1 -> x3, waiting for transfers between devices: 50.8 us -> 127 us  [exchange(): lax.all_to_all(blocks, 'orient', split_axis=0, concat_axis=0, tiled=True)]
    pallas_call x0 -> x3, Pallas kernels: none -> 36.1 us  [the longest x1 20.7 us: per_device(): pl.pallas_call(functools.partial(second_kernel, zt, yt), grid=(zt,), in_s...]
    slice x9 -> x1, local copies, waits for them, and re-layouts: 30.1 us -> 0.99 us  [per_device(): halo_hi = lax.ppermute(q_init[:, :1], 'space', backward)]
    convert_element_type x4 -> x2, other arithmetic: 27.7 us -> 0.02 us  [split3(): return [piece.astype(jnp.bfloat16) for piece in (high, mid, low)]]
    dot_general x4 -> x0, matrix products: 20.8 us -> none  [the longest x1 7.43 us: per_device(): jnp.dot(local_terms, product.reshape(count, -1), precision=lax.Precision....]
    ppermute x4 -> x6, waiting for transfers between devices: 3.41 us -> 23 us  [the longest x1 15.2 us: per_device(): zhi = lax.ppermute(state[0], both, z_prev)]
  transfers between devices with their start and end apart: 6 -> 9, of which waited for: 3 -> 7; matrix products, arithmetic and copies ran while one was open for 2% -> 4% of each run, Pallas kernels for 0% -> 3%
where the time goes in v1:
time: 254 us; the launch traced here: 253 us
  waiting for transfers between devices  150 us (59%)
  Pallas kernels  36.1 us (14%)
  starting transfers between devices  34.1 us (13%)
  local copies, waits for them, and re-layouts  17.6 us (7%)
  blocking collectives  11.5 us (5%)
  other arithmetic  2.85 us (1%)
    all_to_all x3, waiting for transfers between devices, exchange(): lax.all_to_all(blocks, 'orient', split_axis=0, concat_axis=0, tiled=True)  127 us
    all_to_all x3, starting transfers between devices, exchange(): lax.all_to_all(blocks, 'orient', split_axis=0, concat_axis=0, tiled=True)  25.9 us
    pallas_call x1, Pallas kernels, per_device(): pl.pallas_call(functools.partial(second_kernel, zt, yt), grid=(zt,), in_s...  20.7 us
    ppermute x1, waiting for transfers between devices, per_device(): zhi = lax.ppermute(state[0], both, z_prev)  15.2 us
    all_to_all x1, blocking collectives, per_device(): lax.all_to_all(rows, 'orient', split_axis=0, concat_axis=0, axis_index_gr...  11.5 us
    pallas_call x1, Pallas kernels, per_device(): pl.pallas_call(functools.partial(rotate_kernel, yt), grid=(zt,), in_specs...  7.87 us
    pallas_call x1, Pallas kernels, per_device(): pl.pallas_call(functools.partial(advect_kernel, zt, yt), grid=(nzb,), in_...  7.45 us
    unnamed x20, local copies, waits for them, and re-layouts  7.12 us
  transfers between devices with their start and end apart: 9, of which 7 were waited for; matrix products, arithmetic and copies ran while one was open for 4% of the time, Pallas kernels for 3%

profile of v1, /device:TPU:2, one launch (start us, length us, event | category | flops | bytes accessed | tf_op | source)
XLA Modules:
  0.0 252.5 jit_solution(13148311928104873065)
XLA Ops:
  0.6 1.0 fusion.4
  1.6 1.6 collective-permute-start.1
  3.3 0.0 collective-permute-start
  3.3 0.7 abs_multiply_fusion
  4.0 0.8 slice_multiply_fusion
  4.8 0.0 copy-start.7
  4.8 0.1 concatenate.18
  5.0 0.0 copy-done.6
  5.0 0.1 dynamic-slice_bitcast_fusion
  5.1 0.1 copy.24.coef_ref
  5.1 1.2 collective-permute-done.1.hhi_ref
  6.4 2.8 %collective-permute-done.hlo_ref = bf16[4,1,128,128]{3,2,1,0:T(8,128)(2,1)S(1)} collective-permute-done((bf16[4,1,128,128]{3,2,1,0:T(8,128)(2,1)S(1)}, bf16[4,1,128,128]{3,2,1,0:T(8,128)(2,1)S(1)}, u32[]{:S(2)}, u32[]{:S(2)}) %collective-permute-start) | collective-permute-done | bytes 131104 | tf_op jit(solution)/shard_map/ppermute | solution.py:181
  9.2 1.6 copy-done
  10.8 1.9 copy-done.4
  12.6 7.5 %advect.1 = bf16[8,8,4,2,16,128]{5,4,3,2,1,0:T(8,128)(2,1)} custom-call(f32[4,16]{1,0:T(4,128)S(1)} %copy.24.coef_ref, bf16[4,16,128,128]{3,2,1,0:T(8,128)(2,1)S(1)} %copy-done, bf16[4,16,128,128]{3,2,1,0:T(8,128)(2,1)S(1)} %copy-done, bf16[4,16,128,128]{3,2,1,0:T(8,128)(2,1)S(1)} %copy-done, bf16[4,1,128,128]{3,2,1,0:T(8,128)(2,1)S(1)} %collective-permute-done.hlo_ref, ...), custom_call_target="tpu_custom_call" | custom-call | tf_op jit(solution)/shard_map/advect/pallas_call | solution.py:185
  20.1 13.2 %all-to-all-start = ((bf16[64,4,2,16,128]{4,3,2,1,0:T(8,128)(2,1)}), bf16[64,4,2,16,128]{4,3,2,1,0:T(8,128)(2,1)S(1)}, u32[]{:S(2)}, u32[]{:S(2)}) async-start(bf16[64,4,2,16,128]{4,3,2,1,0:T(8,128)(2,1)} %bitcast.2), calls=%async_computation | async-start | bytes 4194304 | tf_op jit(solution)/shard_map/all_to_all | solution.py:204
  33.3 3.5 %copy.28 = bf16[8,8,4,2,16,128]{5,4,3,2,1,0:T(8,128)(2,1)} copy(bf16[8,8,4,2,16,128]{5,4,0,3,1,2:T(8,128)(2,1)} %bitcast.42) | data formatting | bytes 4194304 | tf_op jit(solution)/shard_map/transpose | solution.py:206
  36.8 46.3 %all-to-all-done = bf16[64,4,2,16,128]{4,3,2,1,0:T(8,128)(2,1)S(1)} async-done(((bf16[64,4,2,16,128]{4,3,2,1,0:T(8,128)(2,1)}), bf16[64,4,2,16,128]{4,3,2,1,0:T(8,128)(2,1)S(1)}, u32[]{:S(2)}, u32[]{:S(2)}) %all-to-all-start) | async-done | bytes 2097184 | tf_op jit(solution)/shard_map/all_to_all | solution.py:204
  83.2 1.3 copy-done.2
  84.5 6.2 %all-to-all-start.1 = ((bf16[64,4,2,16,128]{4,3,2,1,0:T(8,128)(2,1)}), bf16[64,4,2,16,128]{4,3,2,1,0:T(8,128)(2,1)}, u32[]{:S(2)}, u32[]{:S(2)}) async-start(bf16[64,4,2,16,128]{4,3,2,1,0:T(8,128)(2,1)} %bitcast.40), calls=%async_computation.1 | async-start | bytes 4194304 | tf_op jit(solution)/shard_map/all_to_all | solution.py:204
  90.7 0.0 copy-start.3
  90.8 1.6 copy-done.3
  92.3 7.9 %rotate.1.q_ref = bf16[2,16,256,128]{3,2,1,0:T(8,128)(2,1)S(1)} custom-call(bf16[256,256]{1,0:T(8,128)(2,1)S(1)} %copy-done.5, bf16[256,2,16,128]{3,2,1,0:T(8,128)(2,1)S(1)} %bitcast.38), custom_call_target="tpu_custom_call" | custom-call | tf_op jit(solution)/shard_map/rotate/pallas_call | solution.py:210
  100.2 0.0 copy-start.1
  100.2 0.0 copy-start.8
  100.2 1.6 slice_bitcast_fusion
  101.9 3.2 %collective-permute-start.3 = (bf16[16,256,128]{2,1,0:T(8,128)(2,1)}, bf16[16,256,128]{2,1,0:T(8,128)(2,1)S(1)}, u32[]{:S(2)}, u32[]{:S(2)}) collective-permute-start(bf16[16,256,128]{2,1,0:T(8,128)(2,1)} %get-tuple-element.10), channel_id=1, source_target_pairs={{1,0},{2,1},{3,2},{4,3},{5,4},{6,5},{7,6},{64,7},{9,8},{10,9},{11,... | collective-permute-start | bytes 3145736 | tf_op jit(solution)/shard_map/ppermute | solution.py:240
  105.1 0.0 collective-permute-start.2
  105.2 0.6 pad_maximum_fusion.1
  105.8 0.8 constant_dynamic-slice_fusion
  106.6 3.3 %collective-permute-start.5 = (bf16[2,256,128]{2,1,0:T(8,128)(2,1)S(1)}, bf16[2,256,128]{2,1,0:T(8,128)(2,1)S(1)}, u32[]{:S(2)}, u32[]{:S(2)}) collective-permute-start(bf16[2,256,128]{2,1,0:T(8,128)(2,1)S(1)} %get-tuple-element.8), channel_id=1, source_target_pairs={{8,0},{9,1},{10,2},{11,3},{12,4},{13,5},{14,6},{15,7},{16,8},{17,9... | collective-permute-start | bytes 393224 | tf_op jit(solution)/shard_map/ppermute | solution.py:242
  109.9 0.0 collective-permute-start.4
  109.9 0.7 pad_maximum_fusion.3
  110.6 0.8 copy.29.ft_ref
  111.5 30.2 %all-to-all-done.1 = bf16[64,4,2,16,128]{4,3,2,1,0:T(8,128)(2,1)} async-done(((bf16[64,4,2,16,128]{4,3,2,1,0:T(8,128)(2,1)}), bf16[64,4,2,16,128]{4,3,2,1,0:T(8,128)(2,1)}, u32[]{:S(2)}, u32[]{:S(2)}) %all-to-all-start.1) | async-done | bytes 2097184 | tf_op jit(solution)/shard_map/all_to_all | solution.py:204
  141.7 0.0 collective-permute-done.5.yhi_ref
  141.7 0.0 collective-permute-done.4.ylo_ref
  141.7 15.2 %collective-permute-done.3.zhi_ref = bf16[16,256,128]{2,1,0:T(8,128)(2,1)S(1)} collective-permute-done((bf16[16,256,128]{2,1,0:T(8,128)(2,1)}, bf16[16,256,128]{2,1,0:T(8,128)(2,1)S(1)}, u32[]{:S(2)}, u32[]{:S(2)}) %collective-permute-start.3) | collective-permute-done | bytes 1048608 | tf_op jit(solution)/shard_map/ppermute | solution.py:240
  156.9 3.8 %collective-permute-done.2.zlo_ref = bf16[16,256,128]{2,1,0:T(8,128)(2,1)} collective-permute-done((bf16[16,256,128]{2,1,0:T(8,128)(2,1)}, bf16[16,256,128]{2,1,0:T(8,128)(2,1)}, u32[]{:S(2)}, u32[]{:S(2)}) %collective-permute-start.2) | collective-permute-done | bytes 1048608 | tf_op jit(solution)/shard_map/ppermute | solution.py:239
  160.7 0.3 broadcast_in_dim.9.coef_ref
  161.0 20.7 %second.1 = (bf16[256,2,16,128]{3,2,1,0:T(8,128)(2,1)}, f32[2,16,8,128]{3,2,1,0:T(8,128)S(1)}) custom-call(bf16[256,256]{1,0:T(8,128)(2,1)S(1)} %copy-done.5, f32[7,256,128]{2,1,0:T(8,128)S(1)} %broadcast_in_dim.9.coef_ref, bf16[256,24]{1,0:T(8,128)(2,1)S(1)} %copy.29.ft_ref, bf16[24,256]{1,0:T(8,128)(2,1)S(1)} %pad_maximum_fusion.2.tt_ref, ...), custom_call_target="tpu_custom_call" | custom-call | tf_op jit(solution)/shard_map/second/pallas_call | solution.py:255
  181.7 0.1 copy.39
  181.8 11.5 %all_to_all.20 = f32[8,6,2,2,128]{4,3,2,1,0:T(2,128)S(1)} all-to-all(f32[8,6,2,2,128]{4,3,2,1,0:T(2,128)S(1)} %bitcast.45), channel_id=1, replica_groups={{0,1,2,3,4,5,6,7},{8,9,10,11,12,13,14,15},{16,17,18,19,20,21,22,23},{24..., dimensions={0} | all-to-all | bytes 196608 | tf_op jit(solution)/shard_map/all_to_all | solution.py:296
  193.3 6.5 %all-to-all-start.2 = ((bf16[64,4,2,16,128]{4,3,2,1,0:T(8,128)(2,1)}), bf16[64,4,2,16,128]{4,3,2,1,0:T(8,128)(2,1)S(1)}, u32[]{:S(2)}, u32[]{:S(2)}) async-start(bf16[64,4,2,16,128]{4,3,2,1,0:T(8,128)(2,1)} %bitcast.13), calls=%async_computation.2 | async-start | bytes 4194304 | tf_op jit(solution)/shard_map/all_to_all | solution.py:204
  199.7 0.1 copy.32
  199.8 0.7 copy.33
  200.5 50.1 %all-to-all-done.2 = bf16[64,4,2,16,128]{4,3,2,1,0:T(8,128)(2,1)S(1)} async-done(((bf16[64,4,2,16,128]{4,3,2,1,0:T(8,128)(2,1)}), bf16[64,4,2,16,128]{4,3,2,1,0:T(8,128)(2,1)S(1)}, u32[]{:S(2)}, u32[]{:S(2)}) %all-to-all-start.2) | async-done | bytes 2097184 | tf_op jit(solution)/shard_map/all_to_all | solution.py:204
  250.6 1.9 copy.30
  (22 shorter events, 0.2 us)
Async XLA Ops:
  1.6 4.7 %collective-permute-start.1 = (bf16[4,1,128,128]{3,2,1,0:T(8,128)(2,1)S(1)}, bf16[4,1,128,128]{3,2,1,0:T(8,128)(2,1)S(1)}, u32[]{:S(2)}, u32[]{:S(2)}) collective-permute-start(bf16[4,1,128,128]{3,2,1,0:T(8,128)(2,1)S(1)} %get-tuple-element.12), channel_id=1, source_target_pairs={{64,0},{128,64},{192,128},{0,192},{65,1},{129,65},{193,129},{1,193... | collective-permute-start | bytes 393224 | tf_op jit(solution)/shard_map/ppermute | solution.py:182
  3.3 5.9 %collective-permute-start = (bf16[4,1,128,128]{3,2,1,0:T(8,128)(2,1)S(1)}, bf16[4,1,128,128]{3,2,1,0:T(8,128)(2,1)S(1)}, u32[]{:S(2)}, u32[]{:S(2)}) collective-permute-start(bf16[4,1,128,128]{3,2,1,0:T(8,128)(2,1)S(1)} %get-tuple-element.13), channel_id=1, source_target_pairs={{0,64},{64,128},{128,192},{192,0},{1,65},{65,129},{129,193},{193,1... | collective-permute-start | bytes 393224 | tf_op jit(solution)/shard_map/ppermute | solution.py:181
  4.0 1.0 copy-start.6
  4.8 15.3 %copy-start.7 = (f32[1,256]{1,0:T(1,128)}, f32[1,256]{1,0:T(1,128)S(1)}, u32[]{:S(2)}) copy-start(f32[1,256]{1,0:T(1,128)S(1)} %fusion.2) | copy-start | bytes 3076
  9.2 1.6 copy-start
  10.8 1.9 copy-start.4
  20.1 63.1 %all-to-all-start = ((bf16[64,4,2,16,128]{4,3,2,1,0:T(8,128)(2,1)}), bf16[64,4,2,16,128]{4,3,2,1,0:T(8,128)(2,1)S(1)}, u32[]{:S(2)}, u32[]{:S(2)}) async-start(bf16[64,4,2,16,128]{4,3,2,1,0:T(8,128)(2,1)} %bitcast.2), calls=%async_computation | async-start | bytes 4194304 | tf_op jit(solution)/shard_map/all_to_all | solution.py:204
  83.2 1.3 copy-start.2
  83.2 7.6 %copy-start.5 = (bf16[256,256]{1,0:T(8,128)(2,1)S(1)}, bf16[256,256]{1,0:T(8,128)(2,1)}, u32[]{:S(2)}) copy-start(bf16[256,256]{1,0:T(8,128)(2,1)} %rot_ref.3) | copy-start | bytes 393220
  84.5 57.2 %all-to-all-start.1 = ((bf16[64,4,2,16,128]{4,3,2,1,0:T(8,128)(2,1)}), bf16[64,4,2,16,128]{4,3,2,1,0:T(8,128)(2,1)}, u32[]{:S(2)}, u32[]{:S(2)}) async-start(bf16[64,4,2,16,128]{4,3,2,1,0:T(8,128)(2,1)} %bitcast.40), calls=%async_computation.1 | async-start | bytes 4194304 | tf_op jit(solution)/shard_map/all_to_all | solution.py:204
  90.7 1.6 copy-start.3
  100.2 6.4 %copy-start.1 = (bf16[2,16,256,128]{3,2,1,0:T(8,128)(2,1)}, bf16[2,16,256,128]{3,2,1,0:T(8,128)(2,1)S(1)}, u32[]{:S(2)}) copy-start(bf16[2,16,256,128]{3,2,1,0:T(8,128)(2,1)S(1)} %rotate.1.q_ref) | copy-start | bytes 6291460
  100.2 4.9 %copy-start.8 = (f32[256]{0:T(256)S(1)}, f32[256]{0:T(256)}, u32[]{:S(2)}) copy-start(f32[256]{0:T(256)} %param.10) | copy-start | bytes 3076
  101.9 55.0 %collective-permute-start.3 = (bf16[16,256,128]{2,1,0:T(8,128)(2,1)}, bf16[16,256,128]{2,1,0:T(8,128)(2,1)S(1)}, u32[]{:S(2)}, u32[]{:S(2)}) collective-permute-start(bf16[16,256,128]{2,1,0:T(8,128)(2,1)} %get-tuple-element.10), channel_id=1, source_target_pairs={{1,0},{2,1},{3,2},{4,3},{5,4},{6,5},{7,6},{64,7},{9,8},{10,9},{11,... | collective-permute-start | bytes 3145736 | tf_op jit(solution)/shard_map/ppermute | solution.py:240
  105.1 55.6 %collective-permute-start.2 = (bf16[16,256,128]{2,1,0:T(8,128)(2,1)}, bf16[16,256,128]{2,1,0:T(8,128)(2,1)}, u32[]{:S(2)}, u32[]{:S(2)}) collective-permute-start(bf16[16,256,128]{2,1,0:T(8,128)(2,1)} %get-tuple-element.11), channel_id=1, source_target_pairs={{0,1},{1,2},{2,3},{3,4},{4,5},{5,6},{6,7},{7,64},{8,9},{9,10},{10,... | collective-permute-start | bytes 3145736 | tf_op jit(solution)/shard_map/ppermute | solution.py:239
  106.6 35.1 %collective-permute-start.5 = (bf16[2,256,128]{2,1,0:T(8,128)(2,1)S(1)}, bf16[2,256,128]{2,1,0:T(8,128)(2,1)S(1)}, u32[]{:S(2)}, u32[]{:S(2)}) collective-permute-start(bf16[2,256,128]{2,1,0:T(8,128)(2,1)S(1)} %get-tuple-element.8), channel_id=1, source_target_pairs={{8,0},{9,1},{10,2},{11,3},{12,4},{13,5},{14,6},{15,7},{16,8},{17,9... | collective-permute-start | bytes 393224 | tf_op jit(solution)/shard_map/ppermute | solution.py:242
  109.9 31.8 %collective-permute-start.4 = (bf16[2,256,128]{2,1,0:T(8,128)(2,1)S(1)}, bf16[2,256,128]{2,1,0:T(8,128)(2,1)S(1)}, u32[]{:S(2)}, u32[]{:S(2)}) collective-permute-start(bf16[2,256,128]{2,1,0:T(8,128)(2,1)S(1)} %get-tuple-element.9), channel_id=1, source_target_pairs={{0,8},{1,9},{2,10},{3,11},{4,12},{5,13},{6,14},{7,15},{8,16},{9,17... | collective-permute-start | bytes 393224 | tf_op jit(solution)/shard_map/ppermute | solution.py:241
  193.3 57.3 %all-to-all-start.2 = ((bf16[64,4,2,16,128]{4,3,2,1,0:T(8,128)(2,1)}), bf16[64,4,2,16,128]{4,3,2,1,0:T(8,128)(2,1)S(1)}, u32[]{:S(2)}, u32[]{:S(2)}) async-start(bf16[64,4,2,16,128]{4,3,2,1,0:T(8,128)(2,1)} %bitcast.13), calls=%async_computation.2 | async-start | bytes 4194304 | tf_op jit(solution)/shard_map/all_to_all | solution.py:204

commit v2 on v0

v2 whole, which is shorter than its diff:
```python
import functools

import jax
import jax.numpy as jnp
from jax import lax
from jax.experimental import pallas as pl
from jax.experimental.pallas import tpu as pltpu
from jax.sharding import PartitionSpec as P

step_length = 0.3
relax_rate = 0.5
coupling = 8.0

F32 = jnp.float32
BF16 = jnp.bfloat16
MESH = pl.DeviceIdType.MESH
ZT = 2
YT = 16
CHUNKS = 4


def whole_kernel(
    dims,
    q_hbm,
    part_hbm,
    w_hbm,
    ub_ref,
    rot_ref,
    dirs,
    weight,
    out_hbm,
    nf_hbm,
    qext,
    wv,
    send1,
    recv1,
    ext,
    wide,
    precv,
    send2,
    nfb,
    cf,
    ft3,
    wown,
    acc,
    sem_in,
    sem_hq,
    sem_hqs,
    sem_r1,
    sem_s1,
    sem_rp,
    sem_sp,
    sem_hz,
    sem_hzs,
    sem_hy,
    sem_hys,
    sem_r2,
    sem_s2,
    sem_rn,
    sem_sn,
):
    spaces, groups, nzb, nyb, count, nz, ny, nx = dims
    no = groups * count
    zt, yt = ZT, YT
    per = yt // CHUNKS
    me = lax.axis_index("orient")
    sp = lax.axis_index("space")
    my_zb = me // nyb
    my_yb = me % nyb
    sp_next = lax.rem(sp + 1, spaces)
    sp_prev = lax.rem(sp + spaces - 1, spaces)
    up = my_zb + 1
    z_next = (lax.rem(sp + up // nzb, spaces), lax.rem(up, nzb) * nyb + my_yb)
    down = my_zb + nzb - 1
    z_prev = (
        lax.rem(sp + spaces - 1 + down // nzb, spaces),
        lax.rem(down, nzb) * nyb + my_yb,
    )
    y_next = (sp, my_zb * nyb + lax.rem(my_yb + 1, nyb))
    y_prev = (sp, my_zb * nyb + lax.rem(my_yb + nyb - 1, nyb))

    load_q = pltpu.make_async_copy(q_hbm, qext.at[:, pl.ds(1, nz)], sem_in.at[0])
    load_w = pltpu.make_async_copy(w_hbm, wv, sem_in.at[1])
    load_q.start()
    load_w.start()

    barrier = pltpu.get_barrier_semaphore()

    def greet(i, carry):
        peer = lax.rem(me + i, groups)
        pl.semaphore_signal(barrier, 1, device_id=(sp, peer), device_id_type=MESH)
        return carry

    for target in (z_next, z_prev, (sp_next, me), (sp_prev, me)):
        pl.semaphore_signal(barrier, 1, device_id=target, device_id_type=MESH)
    lax.fori_loop(1, groups, greet, 0)
    pl.semaphore_wait(barrier, groups + 3)

    def remote(src, dst, ssem, rsem, target):
        return pltpu.make_async_remote_copy(
            src_ref=src,
            dst_ref=dst,
            send_sem=ssem,
            recv_sem=rsem,
            device_id=target,
            device_id_type=MESH,
        )

    remote(
        q_hbm.at[:, pl.ds(nz - 1, 1)], qext.at[:, pl.ds(0, 1)], sem_hqs, sem_hq.at[0], (sp_next, me)
    ).start()
    remote(
        q_hbm.at[:, pl.ds(0, 1)], qext.at[:, pl.ds(nz + 1, 1)], sem_hqs, sem_hq.at[1], (sp_prev, me)
    ).start()

    load_q.wait()
    load_w.wait()

    for p in range(zt):

        def advect_plane(i, carry, p=p):
            zb = lax.rem(my_zb + 1 + i, nzb)
            z = zb * zt + p
            if p == 0:

                @pl.when(zb == 0)
                def low_halo():
                    pltpu.make_async_copy(
                        qext.at[:, pl.ds(0, 1)], qext.at[:, pl.ds(0, 1)], sem_hq.at[0]
                    ).wait()

            if p == zt - 1:

                @pl.when(zb == nzb - 1)
                def high_halo():
                    pltpu.make_async_copy(
                        qext.at[:, pl.ds(nz + 1, 1)], qext.at[:, pl.ds(nz + 1, 1)], sem_hq.at[1]
                    ).wait()

            planes = [wv[c, z].astype(F32) for c in range(6)]
            for o in range(count):
                ux = dirs[0, me * count + o]
                uy = dirs[1, me * count + o]
                uz = dirs[2, me * count + o]
                ax = step_length * jnp.maximum(ux, -ux)
                ay = step_length * jnp.maximum(uy, -uy)
                az = step_length * jnp.maximum(uz, -uz)
                terms = (ux * ux, uy * uy, uz * uz, 2.0 * ux * uy, 2.0 * ux * uz, 2.0 * uy * uz)
                f = qext[o, z + 1].astype(F32)
                below = qext[o, z].astype(F32)
                above = qext[o, z + 2].astype(F32)
                up_x = jnp.where(ux > 0.0, pltpu.roll(f, 1, 1), pltpu.roll(f, nx - 1, 1))
                up_y = jnp.where(uy > 0.0, pltpu.roll(f, 1, 0), pltpu.roll(f, ny - 1, 0))
                up_z = jnp.where(uz > 0.0, below, above)
                moved = f * (1.0 - (ax + ay + az)) + ax * up_x + ay * up_y + az * up_z
                power = (-step_length * terms[0]) * planes[0]
                for c in range(1, 6):
                    power = power + (-step_length * terms[c]) * planes[c]
                res = (moved * jnp.exp(power)).astype(BF16)
                for yb in range(nyb):
                    send1[p, zb * nyb + yb, o] = res[yb * yt : (yb + 1) * yt]

            def ship(j, inner):
                yb = lax.rem(my_yb + 1 + j, nyb)
                d = zb * nyb + yb

                @pl.when(d == me)
                def keep():
                    pltpu.make_async_copy(send1.at[p, d], recv1.at[p, me], sem_r1.at[p]).start()

                @pl.when(d != me)
                def send():
                    remote(
                        send1.at[p, d], recv1.at[p, me], sem_s1, sem_r1.at[p], (sp, d)
                    ).start()

                return inner

            lax.fori_loop(0, nyb, ship, 0)
            return carry

        lax.fori_loop(0, nzb, advect_plane, 0)

    def part_block(d):
        return part_hbm.at[:, pl.ds((d // nyb) * zt, zt), pl.ds(lax.rem(d, nyb) * yt, yt)]

    def ship_part(i, carry):
        d = lax.rem(me + i, groups)
        remote(part_block(d), precv.at[me], sem_sp, sem_rp, (sp, d)).start()
        return carry

    lax.fori_loop(1, groups, ship_part, 0)
    pltpu.make_async_copy(part_block(me), precv.at[me], sem_rp).start()

    ux = ub_ref[0]
    uy = ub_ref[1]
    uz = ub_ref[2]
    ax = step_length * jnp.abs(ux)
    ay = step_length * jnp.abs(uy)
    az = step_length * jnp.abs(uz)
    cf[0] = 1.0 - (ax + ay + az)
    cf[1] = ax
    cf[2] = ay
    cf[3] = az
    lane = lax.broadcasted_iota(jnp.int32, (no, nx), 1)
    terms = (ux * ux, uy * uy, uz * uz, 2.0 * ux * uy, 2.0 * ux * uz, 2.0 * uy * uz)
    packed = jnp.zeros((no, nx), F32)
    for c in range(6):
        value = -step_length * terms[c]
        high = value.astype(BF16).astype(F32)
        rest = value - high
        mid = rest.astype(BF16).astype(F32)
        low = rest - mid
        packed = jnp.where(lane == c, high, packed)
        packed = jnp.where(lane == 8 + c, mid, packed)
        packed = jnp.where(lane == 16 + c, low, packed)
    ft3[...] = packed.astype(BF16)

    wown[...] = jnp.zeros_like(wown)
    for p in range(zt):
        for c in range(6):
            block = wv[c, my_zb * zt + p, pl.ds(pl.multiple_of(my_yb * yt, yt), yt)]
            wown[pl.ds(p * yt * 8 + c, yt, stride=8), :] = block.astype(F32)

    for p in range(zt):
        pltpu.make_async_copy(recv1.at[p], recv1.at[p], sem_r1.at[p]).wait()

        def widen(s, carry, p=p):
            rows = count * yt
            wide[pl.ds(pl.multiple_of(s * rows, rows), rows), :] = (
                recv1[p, s].astype(F32).reshape(rows, nx)
            )
            return carry

        lax.fori_loop(0, groups, widen, 0, unroll=4)
        for chunk in range(CHUNKS):

            def turn(k, carry, p=p, chunk=chunk):
                y = chunk * per + k
                tile = wide[pl.ds(y, no, stride=yt), :].astype(BF16)
                turned = jnp.dot(rot_ref[...], tile, preferred_element_type=F32)
                ext[p + 1, y + 1] = turned.astype(BF16)
                return carry

            lax.fori_loop(0, per, turn, 0, unroll=2)
            rows = pl.ds(1 + chunk * per, per)
            if p == 0:
                remote(
                    ext.at[1, rows], ext.at[zt + 1, rows], sem_hzs, sem_hz.at[1, chunk], z_prev
                ).start()
            if p == zt - 1:
                remote(
                    ext.at[zt, rows], ext.at[0, rows], sem_hzs, sem_hz.at[0, chunk], z_next
                ).start()
            if chunk == 0:
                remote(
                    ext.at[p + 1, pl.ds(1, 1)],
                    ext.at[p + 1, pl.ds(yt + 1, 1)],
                    sem_hys,
                    sem_hy.at[1, p],
                    y_prev,
                ).start()
            if chunk == CHUNKS - 1:
                remote(
                    ext.at[p + 1, pl.ds(yt, 1)],
                    ext.at[p + 1, pl.ds(0, 1)],
                    sem_hys,
                    sem_hy.at[0, p],
                    y_next,
                ).start()

    for p in reversed(range(zt)):
        for side, row in ((0, 0), (1, yt + 1)):
            face = ext.at[p + 1, pl.ds(row, 1)]
            pltpu.make_async_copy(face, face, sem_hy.at[side, p]).wait()
        for chunk in range(CHUNKS):
            rows = pl.ds(1 + chunk * per, per)
            if p == zt - 1:
                face = ext.at[zt + 1, rows]
                pltpu.make_async_copy(face, face, sem_hz.at[1, chunk]).wait()
            if p == 0:
                face = ext.at[0, rows]
                pltpu.make_async_copy(face, face, sem_hz.at[0, chunk]).wait()

            def step(k, carry, p=p, chunk=chunk):
                y = chunk * per + k
                f = ext[p + 1, y + 1].astype(F32)
                up_x = jnp.where(ub_ref[0] > 0.0, pltpu.roll(f, 1, 1), pltpu.roll(f, nx - 1, 1))
                up_y = jnp.where(
                    ub_ref[1] > 0.0, ext[p + 1, y].astype(F32), ext[p + 1, y + 2].astype(F32)
                )
                up_z = jnp.where(
                    ub_ref[2] > 0.0, ext[p, y + 1].astype(F32), ext[p + 2, y + 1].astype(F32)
                )
                moved = f * cf[0] + cf[1] * up_x + cf[2] * up_y + cf[3] * up_z
                w8 = wown[pl.ds(pl.multiple_of((p * yt + y) * 8, 8), 8), :]
                w24 = jnp.concatenate([w8, w8, w8], axis=0).astype(BF16)
                power = jnp.dot(ft3[:, :24], w24, preferred_element_type=F32)
                adv = (moved * jnp.exp(power)).astype(BF16)
                turned = jnp.dot(rot_ref[...], adv, preferred_element_type=F32)
                wide[pl.ds(y, no, stride=yt), :] = turned
                return carry

            lax.fori_loop(0, per, step, 0)

        def ship_home(i, carry, p=p):
            d = lax.rem(me + 1 + i, groups)
            rows = count * yt
            block = wide[pl.ds(pl.multiple_of(d * rows, rows), rows), :]
            send2[p, d] = block.astype(BF16).reshape(count, yt, nx)
            home = out_hbm.at[:, my_zb * zt + p, pl.ds(pl.multiple_of(my_yb * yt, yt), yt)]

            @pl.when(d == me)
            def keep():
                pltpu.make_async_copy(send2.at[p, d], home, sem_r2).start()

            @pl.when(d != me)
            def send():
                remote(send2.at[p, d], home, sem_s2, sem_r2, (sp, d)).start()

            return carry

        lax.fori_loop(0, groups, ship_home, 0)

    pltpu.make_async_copy(precv, precv, sem_rp).wait()
    for p in range(zt):

        def add_terms(d, sums, p=p):
            sums = list(sums)
            for o in range(count):
                gx = dirs[0, d * count + o]
                gy = dirs[1, d * count + o]
                gz = dirs[2, d * count + o]
                gw = weight[d * count + o]
                third = 1.0 / 3.0
                factors = (
                    (gx * gx - third) * gw,
                    (gy * gy - third) * gw,
                    (gz * gz - third) * gw,
                    gx * gy * gw,
                    gx * gz * gw,
                    gy * gz * gw,
                )
                prod = send2[p, d, o].astype(F32) * precv[d, o, p].astype(F32)
                for c in range(6):
                    sums[c] = sums[c] + factors[c] * prod
            return tuple(sums)

        sums = lax.fori_loop(
            0, groups, add_terms, tuple(jnp.zeros((yt, nx), F32) for c in range(6))
        )
        for c in range(6):
            old = wv[c, my_zb * zt + p, pl.ds(pl.multiple_of(my_yb * yt, yt), yt)].astype(F32)
            acc[...] = (1.0 - relax_rate) * old + relax_rate * coupling * sums[c]
            for j in range(nyb):
                nfb[j, c, p] = acc[pl.ds(2 * j, 2), :]

    nf_home = nf_hbm.at[:, pl.ds(my_zb * zt, zt)]

    def ship_field(j, carry):
        k = my_yb * nyb + j

        @pl.when(k == me)
        def keep():
            pltpu.make_async_copy(nfb.at[j], nf_home, sem_rn).start()

        @pl.when(k != me)
        def send():
            remote(nfb.at[j], nf_home, sem_sn, sem_rn, (sp, k)).start()

        return carry

    lax.fori_loop(0, nyb, ship_field, 0)

    def drain(ref, sem):
        pltpu.make_async_copy(ref, ref, sem).wait()

    drain(nf_hbm, sem_rn)
    drain(out_hbm, sem_r2)
    drain(qext.at[:, pl.ds(0, 2)], sem_hqs)
    drain(send1.at[0, pl.ds(0, groups - 1)], sem_s1)
    drain(send1.at[1, pl.ds(0, groups - 1)], sem_s1)
    drain(precv.at[pl.ds(0, groups - 1)], sem_sp)
    drain(ext.at[pl.ds(0, 2), pl.ds(1, yt)], sem_hzs)
    drain(ext.at[0, pl.ds(0, 4)], sem_hys)
    drain(send2.at[0, pl.ds(0, groups - 1)], sem_s2)
    drain(send2.at[1, pl.ds(0, groups - 1)], sem_s2)

    sent_self = my_zb == my_yb

    @pl.when(sent_self)
    def drain_most():
        drain(nfb.at[pl.ds(0, nyb - 1)], sem_sn)

    @pl.when(jnp.logical_not(sent_self))
    def drain_all():
        drain(nfb, sem_sn)


def per_device(q_init, partner, field, orientations, orient_weight, rotation):
    count, nz, ny, nx = q_init.shape
    no = orientations.shape[1]
    nzb, nyb = nz // ZT, ny // YT
    groups = lax.axis_size("orient")
    spaces = lax.axis_size("space")
    dims = (spaces, groups, nzb, nyb, count, nz, ny, nx)
    pairs = ny // groups
    along = jnp.broadcast_to(orientations[:, :, None], (3, no, nx))
    hbm = pl.BlockSpec(memory_space=pl.ANY)
    vmem = pl.BlockSpec(memory_space=pltpu.VMEM)
    smem = pl.BlockSpec(memory_space=pltpu.SMEM)
    dma = pltpu.SemaphoreType.DMA
    return pl.pallas_call(
        functools.partial(whole_kernel, dims),
        in_specs=[hbm, hbm, hbm, vmem, vmem, smem, smem],
        out_specs=[hbm, hbm],
        out_shape=[
            jax.ShapeDtypeStruct((count, nz, ny, nx), BF16),
            jax.ShapeDtypeStruct((6, nz, pairs, nx), F32),
        ],
        scratch_shapes=[
            pltpu.VMEM((count, nz + 2, ny, nx), BF16),
            pltpu.VMEM((6, nz, ny, nx), BF16),
            pltpu.VMEM((ZT, groups, count, YT, nx), BF16),
            pltpu.VMEM((ZT, groups, count, YT, nx), BF16),
            pltpu.VMEM((ZT + 2, YT + 2, no, nx), BF16),
            pltpu.VMEM((no * YT, nx), F32),
            pltpu.VMEM((groups, count, ZT, YT, nx), BF16),
            pltpu.VMEM((ZT, groups, count, YT, nx), BF16),
            pltpu.VMEM((nyb, 6, ZT, pairs, nx), F32),
            pltpu.VMEM((4, no, nx), F32),
            pltpu.VMEM((no, nx), BF16),
            pltpu.VMEM((ZT * YT * 8, nx), F32),
            pltpu.VMEM((YT, nx), F32),
            dma((2,)),
            dma((2,)),
            dma(()),
            dma((ZT,)),
            dma(()),
            dma(()),
            dma(()),
            dma((2, CHUNKS)),
            dma(()),
            dma((2, ZT)),
            dma(()),
            dma(()),
            dma(()),
            dma(()),
            dma(()),
        ],
        compiler_params=pltpu.CompilerParams(
            collective_id=0, has_side_effects=True, vmem_limit_bytes=52 << 20
        ),
        name="whole",
    )(q_init, partner, field, along, rotation, orientations, orient_weight)


def solution(mesh):
    in_specs = (
        P("orient", "space", None, None),
        P("orient", "space", None, None),
        P(None, "space", None, None),
        P(),
        P(),
        P(),
    )
    out_specs = (P("orient", "space", None, None), P(None, "space", "orient", None))
    return jax.shard_map(
        per_device, mesh=mesh, in_specs=in_specs, out_specs=out_specs, check_vma=False
    )
```

time: 732 us -> 170 us (0.23); the launches traced: 721 us -> 169 us
  waiting for transfers between devices: 373 us -> 0 us
  blocking collectives: 177 us -> 0 us
  Pallas kernels: 0 us -> 161 us
  local copies, waits for them, and re-layouts: 89.9 us -> 6.91 us
  other arithmetic: 32.1 us -> 0 us
  matrix products: 20.8 us -> 0 us
  between operations: 14.6 us -> 0.66 us
  starting transfers between devices: 13.6 us -> 0 us
    reduce_scatter x1 -> x0, waiting for transfers between devices: 319 us -> none  [per_device(): lax.psum_scatter(partial_sum, 'orient', scatter_dimension=2, tiled=True)]
    all_to_all x3 -> x0, blocking collectives: 177 us -> none  [the longest x1 63.6 us: per_device(): lax.all_to_all(advance(state), 'orient', split_axis=2, concat_axis=0, til...]
    pallas_call x0 -> x1, Pallas kernels: none -> 161 us  [per_device(): pl.pallas_call(functools.partial(whole_kernel, dims), in_specs=[hbm, hbm,...]
    all_to_all x1 -> x0, waiting for transfers between devices: 50.8 us -> none  [send_back(): lax.all_to_all(turned, 'orient', split_axis=0, concat_axis=2, tiled=True)]
    slice x9 -> x0, local copies, waits for them, and re-layouts: 30.1 us -> none  [the longest x4 20 us: upwind(): fore_x = jnp.roll(center, -1, axis=-1) - center]
    convert_element_type x4 -> x0, other arithmetic: 27.7 us -> none  [the longest x2 27 us: advance(): return (moved * damping).astype(jnp.bfloat16)]
    dot_general x4 -> x0, matrix products: 20.8 us -> none  [the longest x1 7.43 us: per_device(): jnp.dot(local_terms, product.reshape(count, -1), precision=lax.Precision....]
    reshape x4 -> x0, local copies, waits for them, and re-layouts: 18.1 us -> none  [the longest x2 9.18 us: rotate(): return jnp.dot(rotation, flat, preferred_element_type=jnp.float32).astype...]
  transfers between devices with their start and end apart: 6 -> 0, of which waited for: 3 -> 0; matrix products, arithmetic and copies ran while one was open for 2% -> 0% of each run, Pallas kernels for 0% -> 0%
where the time goes in v2:
time: 170 us; the launch traced here: 169 us
  Pallas kernels  161 us (95%)
  local copies, waits for them, and re-layouts  6.91 us (4%)
    pallas_call x1, Pallas kernels, per_device(): pl.pallas_call(functools.partial(whole_kernel, dims), in_specs=[hbm, hbm,...  161 us
    unnamed x8, local copies, waits for them, and re-layouts  6.07 us

profile of v2, /device:TPU:2, one launch (start us, length us, event | category | flops | bytes accessed | tf_op | source)
XLA Modules:
  0.0 168.6 jit_solution(11396796192141424750)
XLA Ops:
  0.6 0.8 broadcast_in_dim.2.ub_ref
  1.5 0.0 copy-start
  1.5 0.9 copy-done
  2.4 0.0 copy-start.1
  2.4 0.7 copy-done.1
  3.1 0.0 copy-start.2
  3.1 0.7 copy-done.2
  3.8 161.1 %whole.1 = (bf16[4,16,128,128]{3,2,1,0:T(8,128)(2,1)}, f32[6,16,2,128]{3,2,1,0:T(2,128)S(1)}) custom-call(bf16[4,16,128,128]{3,2,1,0:T(8,128)(2,1)} %q_hbm.1, bf16[4,16,128,128]{3,2,1,0:T(8,128)(2,1)} %part_hbm.1, bf16[6,16,128,128]{3,2,1,0:T(8,128)(2,1)} %w_hbm.1, f32[3,256,128]{2,1,0:T(8,128)S(1)} %broadcast_in_dim.2.ub_ref, bf16[256,256]{1,0:T(8,128)(2,1)S(1)} %copy-done, ...), custom_call_target="tpu_custom_call" | custom-call | tf_op jit(solution)/shard_map/whole/pallas_call | solution.py:413
  164.8 3.2 %copy.10 = bf16[4,16,128,128]{3,2,1,0:T(8,128)(2,1)} copy(bf16[4,16,128,128]{3,2,1,0:T(8,128)(2,1)} %get-tuple-element.4) | data formatting | bytes 4194304
  168.0 0.6 copy.11
Async XLA Ops:
  1.5 0.9 copy-start
  2.4 0.7 copy-start.1
  3.1 0.7 copy-start.2

commit v3 on v2

--- a/solution.py
+++ b/solution.py
@@ -17,6 +17,7 @@
 ZT = 2
 YT = 16
 CHUNKS = 4
+EARLY = 13
 
 
 def whole_kernel(
@@ -24,12 +25,16 @@
     q_hbm,
     part_hbm,
     w_hbm,
-    ub_ref,
+    rot_hbm,
+    dirs_hbm,
+    weight_hbm,
+    out_hbm,
+    nf_hbm,
     rot_ref,
+    dirs_row,
     dirs,
     weight,
-    out_hbm,
-    nf_hbm,
+    ub_ref,
     qext,
     wv,
     send1,
@@ -81,8 +86,16 @@
 
     load_q = pltpu.make_async_copy(q_hbm, qext.at[:, pl.ds(1, nz)], sem_in.at[0])
     load_w = pltpu.make_async_copy(w_hbm, wv, sem_in.at[1])
+    loads = [
+        pltpu.make_async_copy(dirs_hbm, dirs, sem_in.at[2]),
+        pltpu.make_async_copy(dirs_hbm, dirs_row, sem_in.at[3]),
+        pltpu.make_async_copy(weight_hbm, weight, sem_in.at[4]),
+        pltpu.make_async_copy(rot_hbm, rot_ref, sem_in.at[5]),
+    ]
     load_q.start()
     load_w.start()
+    for load in loads:
+        load.start()
 
     barrier = pltpu.get_barrier_semaphore()
 
@@ -113,8 +126,19 @@
         q_hbm.at[:, pl.ds(0, 1)], qext.at[:, pl.ds(nz + 1, 1)], sem_hqs, sem_hq.at[1], (sp_prev, me)
     ).start()
 
+    def part_block(d):
+        return part_hbm.at[:, pl.ds((d // nyb) * zt, zt), pl.ds(lax.rem(d, nyb) * yt, yt)]
+
+    def ship_part(i, carry):
+        d = lax.rem(me + i, groups)
+        remote(part_block(d), precv.at[me], sem_sp, sem_rp, (sp, d)).start()
+        return carry
+
+    lax.fori_loop(1, EARLY, ship_part, 0)
     load_q.wait()
     load_w.wait()
+    for load in loads:
+        load.wait()
 
     for p in range(zt):
 
@@ -181,17 +205,15 @@
 
         lax.fori_loop(0, nzb, advect_plane, 0)
 
-    def part_block(d):
-        return part_hbm.at[:, pl.ds((d // nyb) * zt, zt), pl.ds(lax.rem(d, nyb) * yt, yt)]
-
-    def ship_part(i, carry):
-        d = lax.rem(me + i, groups)
-        remote(part_block(d), precv.at[me], sem_sp, sem_rp, (sp, d)).start()
-        return carry
-
-    lax.fori_loop(1, groups, ship_part, 0)
+    lax.fori_loop(EARLY, groups, ship_part, 0)
     pltpu.make_async_copy(part_block(me), precv.at[me], sem_rp).start()
 
+    diagonal = lax.broadcasted_iota(jnp.int32, (no, no), 0) == lax.broadcasted_iota(
+        jnp.int32, (no, no), 1
+    )
+    for a in range(3):
+        spread = jnp.where(diagonal, jnp.broadcast_to(dirs_row[pl.ds(a, 1), :], (no, no)), 0.0)
+        ub_ref[a] = jnp.broadcast_to(jnp.sum(spread, axis=1, keepdims=True), (no, nx))
     ux = ub_ref[0]
     uy = ub_ref[1]
     uz = ub_ref[2]
@@ -405,20 +427,23 @@
     spaces = lax.axis_size("space")
     dims = (spaces, groups, nzb, nyb, count, nz, ny, nx)
     pairs = ny // groups
-    along = jnp.broadcast_to(orientations[:, :, None], (3, no, nx))
-    hbm = pl.BlockSpec(memory_space=pl.ANY)
-    vmem = pl.BlockSpec(memory_space=pltpu.VMEM)
-    smem = pl.BlockSpec(memory_space=pltpu.SMEM)
+    hbm = pl.BlockSpec(memory_space=pltpu.HBM)
+    anywhere = pl.BlockSpec(memory_space=pltpu.VMEM)
     dma = pltpu.SemaphoreType.DMA
     return pl.pallas_call(
         functools.partial(whole_kernel, dims),
-        in_specs=[hbm, hbm, hbm, vmem, vmem, smem, smem],
-        out_specs=[hbm, hbm],
+        in_specs=[hbm] * 6,
+        out_specs=[anywhere, anywhere],
         out_shape=[
             jax.ShapeDtypeStruct((count, nz, ny, nx), BF16),
             jax.ShapeDtypeStruct((6, nz, pairs, nx), F32),
         ],
         scratch_shapes=[
+            pltpu.VMEM((no, no), BF16),
+            pltpu.VMEM((3, no), F32),
+            pltpu.SMEM((3, no), F32),
+            pltpu.SMEM((no,), F32),
+            pltpu.VMEM((3, no, nx), F32),
             pltpu.VMEM((count, nz + 2, ny, nx), BF16),
             pltpu.VMEM((6, nz, ny, nx), BF16),
             pltpu.VMEM((ZT, groups, count, YT, nx), BF16),
@@ -432,7 +457,7 @@
             pltpu.VMEM((no, nx), BF16),
             pltpu.VMEM((ZT * YT * 8, nx), F32),
             pltpu.VMEM((YT, nx), F32),
-            dma((2,)),
+            dma((6,)),
             dma((2,)),
             dma(()),
             dma((ZT,)),
@@ -449,10 +474,15 @@
             dma(()),
         ],
         compiler_params=pltpu.CompilerParams(
-            collective_id=0, has_side_effects=True, vmem_limit_bytes=52 << 20
+            collective_id=0, has_side_effects=True, vmem_limit_bytes=40 << 20
         ),
         name="whole",
-    )(q_init, partner, field, along, rotation, orientations, orient_weight)
+    )(
+        *[
+            pltpu.with_memory_space_constraint(x, pltpu.HBM)
+            for x in (q_init, partner, field, rotation, orientations, orient_weight)
+        ]
+    )
 
 
 def solution(mesh):

time: 170 us -> 165 us (0.971)
  local copies, waits for them, and re-layouts: 6.91 us -> 1.96 us
    unnamed x8 -> x2, local copies, waits for them, and re-layouts: 6.07 us -> 1.96 us
where the time goes in v3:
time: 165 us; the launch traced here: 164 us
  Pallas kernels  161 us (98%)
  local copies, waits for them, and re-layouts  1.96 us (1%)
    pallas_call x1, Pallas kernels, per_device(): pl.pallas_call(functools.partial(whole_kernel, dims), in_specs=[hbm] * 6,...  161 us

profile of v3, /device:TPU:2, one launch (start us, length us, event | category | flops | bytes accessed | tf_op | source)
XLA Modules:
  0.0 163.8 jit_solution(9328990665732309333)
XLA Ops:
  0.6 161.2 %whole.1 = (bf16[4,16,128,128]{3,2,1,0:T(8,128)(2,1)S(1)}, f32[6,16,2,128]{3,2,1,0:T(2,128)S(1)}) custom-call(bf16[4,16,128,128]{3,2,1,0:T(8,128)(2,1)} %q_hbm.1, bf16[4,16,128,128]{3,2,1,0:T(8,128)(2,1)} %part_hbm.1, bf16[6,16,128,128]{3,2,1,0:T(8,128)(2,1)} %w_hbm.1, bf16[256,256]{1,0:T(8,128)(2,1)} %rot_hbm.1, f32[3,256]{1,0:T(4,128)} %dirs_hbm.1, ...), custom_call_target="tpu_custom_call" | custom-call | tf_op jit(solution)/shard_map/whole/pallas_call | solution.py:433
  161.9 1.3 copy.10
  163.2 0.6 copy.11

commit v4 on v3

--- a/solution.py
+++ b/solution.py
@@ -17,7 +17,11 @@
 ZT = 2
 YT = 16
 CHUNKS = 4
-EARLY = 13
+EARLY = 0
+LATE = 0
+PART_ORDER = (4, 3, 5, 2, 6, 1, 7, 0)
+Z_ORDER = (4, 3, 5, 2, 6, 1, 7, 0)
+XY_ORDER = (4, 3, 5, 2, 6, 1, 7, 0)
 
 
 def whole_kernel(
@@ -41,13 +45,16 @@
     recv1,
     ext,
     wide,
-    precv,
+    pmid,
     send2,
+    mid,
+    pt,
+    rs,
+    tt,
     nfb,
     cf,
     ft3,
     wown,
-    acc,
     sem_in,
     sem_hq,
     sem_hqs,
@@ -59,8 +66,12 @@
     sem_hzs,
     sem_hy,
     sem_hys,
-    sem_r2,
-    sem_s2,
+    sem_rm,
+    sem_sm,
+    sem_ro,
+    sem_so,
+    sem_rt,
+    sem_st,
     sem_rn,
     sem_sn,
 ):
@@ -68,6 +79,7 @@
     no = groups * count
     zt, yt = ZT, YT
     per = yt // CHUNKS
+    half = yt // 2
     me = lax.axis_index("orient")
     sp = lax.axis_index("space")
     my_zb = me // nyb
@@ -126,15 +138,17 @@
         q_hbm.at[:, pl.ds(0, 1)], qext.at[:, pl.ds(nz + 1, 1)], sem_hqs, sem_hq.at[1], (sp_prev, me)
     ).start()
 
-    def part_block(d):
-        return part_hbm.at[:, pl.ds((d // nyb) * zt, zt), pl.ds(lax.rem(d, nyb) * yt, yt)]
-
-    def ship_part(i, carry):
-        d = lax.rem(me + i, groups)
-        remote(part_block(d), precv.at[me], sem_sp, sem_rp, (sp, d)).start()
-        return carry
-
-    lax.fori_loop(1, EARLY, ship_part, 0)
+    def ship_part(i):
+        xy = lax.rem(my_zb + i, nzb)
+        slot = (nzb - i) % nzb
+        src = part_hbm.at[:, pl.ds(xy * zt, zt)]
+        if i == 0:
+            pltpu.make_async_copy(src, pmid.at[slot], sem_rp).start()
+        else:
+            remote(src, pmid.at[slot], sem_sp, sem_rp, (sp, xy * nyb + my_yb)).start()
+
+    for i in PART_ORDER[:EARLY]:
+        ship_part(i)
     load_q.wait()
     load_w.wait()
     for load in loads:
@@ -205,8 +219,8 @@
 
         lax.fori_loop(0, nzb, advect_plane, 0)
 
-    lax.fori_loop(EARLY, groups, ship_part, 0)
-    pltpu.make_async_copy(part_block(me), precv.at[me], sem_rp).start()
+    for i in PART_ORDER[EARLY:LATE]:
+        ship_part(i)
 
     diagonal = lax.broadcasted_iota(jnp.int32, (no, no), 0) == lax.broadcasted_iota(
         jnp.int32, (no, no), 1
@@ -231,10 +245,10 @@
         value = -step_length * terms[c]
         high = value.astype(BF16).astype(F32)
         rest = value - high
-        mid = rest.astype(BF16).astype(F32)
-        low = rest - mid
+        middle = rest.astype(BF16).astype(F32)
+        low = rest - middle
         packed = jnp.where(lane == c, high, packed)
-        packed = jnp.where(lane == 8 + c, mid, packed)
+        packed = jnp.where(lane == 8 + c, middle, packed)
         packed = jnp.where(lane == 16 + c, low, packed)
     ft3[...] = packed.astype(BF16)
 
@@ -291,20 +305,40 @@
                     y_next,
                 ).start()
 
-    for p in reversed(range(zt)):
-        for side, row in ((0, 0), (1, yt + 1)):
-            face = ext.at[p + 1, pl.ds(row, 1)]
-            pltpu.make_async_copy(face, face, sem_hy.at[side, p]).wait()
-        for chunk in range(CHUNKS):
+    for i in PART_ORDER[LATE:]:
+        ship_part(i)
+
+    def factor(i, carry):
+        o = (lax.rem(my_zb + i // count, nzb) * nyb + my_yb) * count + lax.rem(i, count)
+        gx = dirs[0, o]
+        gy = dirs[1, o]
+        gz = dirs[2, o]
+        gw = weight[o]
+        third = 1.0 / 3.0
+        tt[0, i] = (gx * gx - third) * gw
+        tt[1, i] = (gy * gy - third) * gw
+        tt[2, i] = (gz * gz - third) * gw
+        tt[3, i] = gx * gy * gw
+        tt[4, i] = gx * gz * gw
+        tt[5, i] = gy * gz * gw
+        return carry
+
+    lax.fori_loop(0, nzb * count, factor, 0)
+
+    def await_copy(ref, sem):
+        pltpu.make_async_copy(ref, ref, sem).wait()
+
+    def second_step(p, h):
+        face = ext.at[p + 1, pl.ds((yt + 1) * h, 1)]
+        await_copy(face, sem_hy.at[h, p])
+        for chunk in range(h * CHUNKS // 2, (h + 1) * CHUNKS // 2):
             rows = pl.ds(1 + chunk * per, per)
             if p == zt - 1:
-                face = ext.at[zt + 1, rows]
-                pltpu.make_async_copy(face, face, sem_hz.at[1, chunk]).wait()
+                await_copy(ext.at[zt + 1, rows], sem_hz.at[1, chunk])
             if p == 0:
-                face = ext.at[0, rows]
-                pltpu.make_async_copy(face, face, sem_hz.at[0, chunk]).wait()
-
-            def step(k, carry, p=p, chunk=chunk):
+                await_copy(ext.at[0, rows], sem_hz.at[0, chunk])
+
+            def step(k, carry, chunk=chunk):
                 y = chunk * per + k
                 f = ext[p + 1, y + 1].astype(F32)
                 up_x = jnp.where(ub_ref[0] > 0.0, pltpu.roll(f, 1, 1), pltpu.roll(f, nx - 1, 1))
@@ -320,93 +354,120 @@
                 power = jnp.dot(ft3[:, :24], w24, preferred_element_type=F32)
                 adv = (moved * jnp.exp(power)).astype(BF16)
                 turned = jnp.dot(rot_ref[...], adv, preferred_element_type=F32)
-                wide[pl.ds(y, no, stride=yt), :] = turned
+                wide[pl.ds(y - h * half, no, stride=half), :] = turned
                 return carry
 
             lax.fori_loop(0, per, step, 0)
 
-        def ship_home(i, carry, p=p):
-            d = lax.rem(me + 1 + i, groups)
-            rows = count * yt
-            block = wide[pl.ds(pl.multiple_of(d * rows, rows), rows), :]
-            send2[p, d] = block.astype(BF16).reshape(count, yt, nx)
-            home = out_hbm.at[:, my_zb * zt + p, pl.ds(pl.multiple_of(my_yb * yt, yt), yt)]
-
-            @pl.when(d == me)
-            def keep():
-                pltpu.make_async_copy(send2.at[p, d], home, sem_r2).start()
-
-            @pl.when(d != me)
-            def send():
-                remote(send2.at[p, d], home, sem_s2, sem_r2, (sp, d)).start()
-
-            return carry
-
-        lax.fori_loop(0, groups, ship_home, 0)
-
-    pltpu.make_async_copy(precv, precv, sem_rp).wait()
-    for p in range(zt):
-
-        def add_terms(d, sums, p=p):
-            sums = list(sums)
-            for o in range(count):
-                gx = dirs[0, d * count + o]
-                gy = dirs[1, d * count + o]
-                gz = dirs[2, d * count + o]
-                gw = weight[d * count + o]
-                third = 1.0 / 3.0
-                factors = (
-                    (gx * gx - third) * gw,
-                    (gy * gy - third) * gw,
-                    (gz * gz - third) * gw,
-                    gx * gy * gw,
-                    gx * gz * gw,
-                    gy * gz * gw,
-                )
-                prod = send2[p, d, o].astype(F32) * precv[d, o, p].astype(F32)
-                for c in range(6):
-                    sums[c] = sums[c] + factors[c] * prod
-            return tuple(sums)
-
-        sums = lax.fori_loop(
-            0, groups, add_terms, tuple(jnp.zeros((yt, nx), F32) for c in range(6))
-        )
+        for i in Z_ORDER:
+            zc = lax.rem(my_yb + i, nyb)
+
+            def pack(r, carry, zc=zc):
+                d = lax.rem(my_zb + r, nzb) * nyb + zc
+                rows = count * half
+                block = wide[pl.ds(pl.multiple_of(d * rows, rows), rows), :]
+                send2[p, h, zc, r] = block.astype(BF16).reshape(count, half, nx)
+                return carry
+
+            lax.fori_loop(0, nzb, pack, 0, unroll=4)
+            src = send2.at[p, h, zc]
+            dst = mid.at[p, h, :, :, my_yb]
+            if i == 0:
+                pltpu.make_async_copy(src, dst, sem_rm.at[p, h]).start()
+            else:
+                remote(src, dst, sem_sm, sem_rm.at[p, h], (sp, my_zb * nyb + zc)).start()
+
+    def pass_on(p, h):
+        await_copy(mid.at[p, h], sem_rm.at[p, h])
+        home = out_hbm.at[:, my_zb * zt + p, :, h]
+        for r in XY_ORDER:
+            src = mid.at[p, h, r]
+            if r == 0:
+                pltpu.make_async_copy(src, home, sem_ro).start()
+            else:
+                xy = lax.rem(my_zb + r, nzb)
+                remote(src, home, sem_so, sem_ro, (sp, xy * nyb + my_yb)).start()
+        for g in range(2):
+            blocks = pl.ds(g * nyb // 2, nyb // 2)
+
+            def add_terms(i, sums, blocks=blocks):
+                r = i // count
+                o = lax.rem(i, count)
+                prod = mid[p, h, r, o, blocks].astype(F32) * pmid[r, o, p, blocks, h].astype(F32)
+                return tuple(sums[c] + tt[c, i] * prod for c in range(6))
+
+            zero = jnp.zeros((nyb // 2, half, nx), F32)
+            sums = lax.fori_loop(0, nzb * count, add_terms, (zero,) * 6)
+            for c in range(6):
+                pt[p, h, blocks, c] = sums[c]
+        for i in Z_ORDER:
+            zc = lax.rem(my_yb + i, nyb)
+            src = pt.at[p, h, zc]
+            dst = rs.at[p, h, my_yb]
+            if i == 0:
+                pltpu.make_async_copy(src, dst, sem_rt.at[p, h]).start()
+            else:
+                remote(src, dst, sem_st, sem_rt.at[p, h], (sp, my_zb * nyb + zc)).start()
+
+    nf_home = nf_hbm.at[:, pl.ds(my_zb * zt, zt)]
+    each = nyb // 2
+
+    def relax(p, h):
+        await_copy(rs.at[p, h], sem_rt.at[p, h])
         for c in range(6):
+            total = rs[p, h, 0, c]
+            for s in range(1, nyb):
+                total = total + rs[p, h, s, c]
             old = wv[c, my_zb * zt + p, pl.ds(pl.multiple_of(my_yb * yt, yt), yt)].astype(F32)
-            acc[...] = (1.0 - relax_rate) * old + relax_rate * coupling * sums[c]
-            for j in range(nyb):
-                nfb[j, c, p] = acc[pl.ds(2 * j, 2), :]
-
-    nf_home = nf_hbm.at[:, pl.ds(my_zb * zt, zt)]
-
-    def ship_field(j, carry):
-        k = my_yb * nyb + j
-
-        @pl.when(k == me)
-        def keep():
-            pltpu.make_async_copy(nfb.at[j], nf_home, sem_rn).start()
-
-        @pl.when(k != me)
-        def send():
-            remote(nfb.at[j], nf_home, sem_sn, sem_rn, (sp, k)).start()
-
-        return carry
-
-    lax.fori_loop(0, nyb, ship_field, 0)
+            old = old[h * half : (h + 1) * half]
+            value = (1.0 - relax_rate) * old + relax_rate * coupling * total
+            for j in range(each):
+                nfb[h * each + j, c, p] = value[2 * j : 2 * j + 2]
+        if p == 0:
+
+            def ship_field(j, carry):
+                k = my_yb * nyb + j
+
+                @pl.when(k == me)
+                def keep():
+                    pltpu.make_async_copy(nfb.at[j], nf_home, sem_rn).start()
+
+                @pl.when(k != me)
+                def send():
+                    remote(nfb.at[j], nf_home, sem_sn, sem_rn, (sp, k)).start()
+
+                return carry
+
+            lax.fori_loop(h * each, (h + 1) * each, ship_field, 0)
+
+    second_step(1, 0)
+    second_step(1, 1)
+    second_step(0, 0)
+    await_copy(pmid, sem_rp)
+    pass_on(1, 0)
+    second_step(0, 1)
+    pass_on(1, 1)
+    relax(1, 0)
+    pass_on(0, 0)
+    relax(1, 1)
+    pass_on(0, 1)
+    relax(0, 0)
+    relax(0, 1)
 
     def drain(ref, sem):
         pltpu.make_async_copy(ref, ref, sem).wait()
 
     drain(nf_hbm, sem_rn)
-    drain(out_hbm, sem_r2)
+    drain(out_hbm, sem_ro)
     drain(qext.at[:, pl.ds(0, 2)], sem_hqs)
     drain(send1.at[0, pl.ds(0, groups - 1)], sem_s1)
     drain(send1.at[1, pl.ds(0, groups - 1)], sem_s1)
-    drain(precv.at[pl.ds(0, groups - 1)], sem_sp)
+    drain(pmid.at[pl.ds(0, nzb - 1)], sem_sp)
     drain(ext.at[pl.ds(0, 2), pl.ds(1, yt)], sem_hzs)
     drain(ext.at[0, pl.ds(0, 4)], sem_hys)
-    drain(send2.at[0, pl.ds(0, groups - 1)], sem_s2)
-    drain(send2.at[1, pl.ds(0, groups - 1)], sem_s2)
+    drain(send2.at[:, :, pl.ds(0, nyb - 1)], sem_sm)
+    drain(mid.at[:, :, pl.ds(0, nzb - 1)], sem_so)
+    drain(pt.at[:, :, pl.ds(0, nyb - 1)], sem_st)
 
     sent_self = my_zb == my_yb
 
@@ -430,12 +491,13 @@
     hbm = pl.BlockSpec(memory_space=pltpu.HBM)
     anywhere = pl.BlockSpec(memory_space=pltpu.VMEM)
     dma = pltpu.SemaphoreType.DMA
-    return pl.pallas_call(
+    part = partner.reshape(count, nz, nyb, 2, YT // 2, nx)
+    out, new_field = pl.pallas_call(
         functools.partial(whole_kernel, dims),
         in_specs=[hbm] * 6,
         out_specs=[anywhere, anywhere],
         out_shape=[
-            jax.ShapeDtypeStruct((count, nz, ny, nx), BF16),
+            jax.ShapeDtypeStruct((count, nz, nyb, 2, YT // 2, nx), BF16),
             jax.ShapeDtypeStruct((6, nz, pairs, nx), F32),
         ],
         scratch_shapes=[
@@ -450,13 +512,16 @@
             pltpu.VMEM((ZT, groups, count, YT, nx), BF16),
             pltpu.VMEM((ZT + 2, YT + 2, no, nx), BF16),
             pltpu.VMEM((no * YT, nx), F32),
-            pltpu.VMEM((groups, count, ZT, YT, nx), BF16),
-            pltpu.VMEM((ZT, groups, count, YT, nx), BF16),
+            pltpu.VMEM((nzb, count, ZT, nyb, 2, YT // 2, nx), BF16),
+            pltpu.VMEM((ZT, 2, nyb, nzb, count, YT // 2, nx), BF16),
+            pltpu.VMEM((ZT, 2, nzb, count, nyb, YT // 2, nx), BF16),
+            pltpu.VMEM((ZT, 2, nyb, 6, YT // 2, nx), F32),
+            pltpu.VMEM((ZT, 2, nyb, 6, YT // 2, nx), F32),
+            pltpu.SMEM((6, nzb * count), F32),
             pltpu.VMEM((nyb, 6, ZT, pairs, nx), F32),
             pltpu.VMEM((4, no, nx), F32),
             pltpu.VMEM((no, nx), BF16),
             pltpu.VMEM((ZT * YT * 8, nx), F32),
-            pltpu.VMEM((YT, nx), F32),
             dma((6,)),
             dma((2,)),
             dma(()),
@@ -468,7 +533,11 @@
             dma(()),
             dma((2, ZT)),
             dma(()),
-            dma(()),
+            dma((ZT, 2)),
+            dma(()),
+            dma(()),
+            dma(()),
+            dma((ZT, 2)),
             dma(()),
             dma(()),
             dma(()),
@@ -480,9 +549,10 @@
     )(
         *[
             pltpu.with_memory_space_constraint(x, pltpu.HBM)
-            for x in (q_init, partner, field, rotation, orientations, orient_weight)
+            for x in (q_init, part, field, rotation, orientations, orient_weight)
         ]
     )
+    return out.reshape(count, nz, ny, nx), new_field
 
 
 def solution(mesh):

time: 165 us -> 147 us (0.89)
  Pallas kernels: 161 us -> 144 us
    pallas_call x1, Pallas kernels: 161 us -> 144 us  [per_device(): pl.pallas_call(functools.partial(whole_kernel, dims), in_specs=[hbm] * 6,...]
where the time goes in v4:
time: 147 us
  Pallas kernels  144 us (98%)
  local copies, waits for them, and re-layouts  1.96 us (1%)
    pallas_call x1, Pallas kernels, per_device(): pl.pallas_call(functools.partial(whole_kernel, dims), in_specs=[hbm] * 6,...  144 us

profile of v4, /device:TPU:2, one launch (start us, length us, event | category | flops | bytes accessed | tf_op | source)
XLA Modules:
  0.0 146.6 jit_solution(1491559890839332199)
XLA Ops:
  0.6 144.0 %whole.1 = (bf16[4,16,8,2,8,128]{5,4,3,2,1,0:T(8,128)(2,1)S(1)}, f32[6,16,2,128]{3,2,1,0:T(2,128)S(1)}) custom-call(bf16[4,16,128,128]{3,2,1,0:T(8,128)(2,1)} %q_hbm.1, bf16[4,16,8,2,8,128]{5,4,3,2,1,0:T(8,128)(2,1)} %bitcast.3, bf16[6,16,128,128]{3,2,1,0:T(8,128)(2,1)} %w_hbm.1, bf16[256,256]{1,0:T(8,128)(2,1)} %rot_hbm.1, f32[3,256]{1,0:T(4,128)} %dirs_hbm.1, ...), custom_call_target="tpu_custom_call" | custom-call | tf_op jit(solution)/shard_map/whole/pallas_call | solution.py:495
  144.6 1.3 copy.10
  145.9 0.6 copy.11

commit v5 on v4

--- a/solution.py
+++ b/solution.py
@@ -17,9 +17,9 @@
 ZT = 2
 YT = 16
 CHUNKS = 4
+SENT = 5
 EARLY = 0
-LATE = 0
-PART_ORDER = (4, 3, 5, 2, 6, 1, 7, 0)
+WOVEN = 0
 Z_ORDER = (4, 3, 5, 2, 6, 1, 7, 0)
 XY_ORDER = (4, 3, 5, 2, 6, 1, 7, 0)
 
@@ -138,17 +138,27 @@
         q_hbm.at[:, pl.ds(0, 1)], qext.at[:, pl.ds(nz + 1, 1)], sem_hqs, sem_hq.at[1], (sp_prev, me)
     ).start()
 
-    def ship_part(i):
+    def part_piece(i, p):
         xy = lax.rem(my_zb + i, nzb)
-        slot = (nzb - i) % nzb
-        src = part_hbm.at[:, pl.ds(xy * zt, zt)]
-        if i == 0:
-            pltpu.make_async_copy(src, pmid.at[slot], sem_rp).start()
-        else:
-            remote(src, pmid.at[slot], sem_sp, sem_rp, (sp, xy * nyb + my_yb)).start()
-
-    for i in PART_ORDER[:EARLY]:
-        ship_part(i)
+        slot = lax.rem(nzb - i, nzb)
+        return part_hbm.at[:, xy * zt + p], pmid.at[slot, :, p], (sp, xy * nyb + my_yb)
+
+    def ship_part(i, p):
+        src, dst, target = part_piece(i, p)
+        remote(src, dst, sem_sp, sem_rp, target).start()
+
+    for p in range(zt):
+        src, dst, target = part_piece(0, p)
+        pltpu.make_async_copy(src, dst, sem_rp).start()
+
+    def ship_parts(first, last):
+        def one(n, carry):
+            ship_part(1 + n // zt, lax.rem(n, zt))
+            return carry
+
+        lax.fori_loop(first, last, one, 0)
+
+    ship_parts(0, EARLY)
     load_q.wait()
     load_w.wait()
     for load in loads:
@@ -208,19 +218,32 @@
 
                 @pl.when(d != me)
                 def send():
-                    remote(
-                        send1.at[p, d], recv1.at[p, me], sem_s1, sem_r1.at[p], (sp, d)
-                    ).start()
+                    left = sem_s1.at[i if p == 0 else nzb]
+                    remote(send1.at[p, d], recv1.at[p, me], left, sem_r1.at[p], (sp, d)).start()
 
                 return inner
 
+            if p > 0:
+                @pl.when(i < nzb - 1)
+                def others_left():
+                    sent = send1.at[0, pl.ds(0, nyb)]
+                    pltpu.make_async_copy(sent, sent, sem_s1.at[i]).wait()
+
+                @pl.when(i == nzb - 1)
+                def own_left():
+                    sent = send1.at[0, pl.ds(0, nyb - 1)]
+                    pltpu.make_async_copy(sent, sent, sem_s1.at[i]).wait()
+
             lax.fori_loop(0, nyb, ship, 0)
+            turn = p * nzb + i - (zt * nzb - WOVEN)
+
+            @pl.when(turn >= 0)
+            def weave():
+                ship_part(1 + (EARLY + turn) // zt, lax.rem(EARLY + turn, zt))
+
             return carry
 
         lax.fori_loop(0, nzb, advect_plane, 0)
-
-    for i in PART_ORDER[EARLY:LATE]:
-        ship_part(i)
 
     diagonal = lax.broadcasted_iota(jnp.int32, (no, no), 0) == lax.broadcasted_iota(
         jnp.int32, (no, no), 1
@@ -305,8 +328,7 @@
                     y_next,
                 ).start()
 
-    for i in PART_ORDER[LATE:]:
-        ship_part(i)
+    ship_parts(EARLY + WOVEN, (nzb - 1) * zt)
 
     def factor(i, carry):
         o = (lax.rem(my_zb + i // count, nzb) * nyb + my_yb) * count + lax.rem(i, count)
@@ -317,10 +339,9 @@
         third = 1.0 / 3.0
         tt[0, i] = (gx * gx - third) * gw
         tt[1, i] = (gy * gy - third) * gw
-        tt[2, i] = (gz * gz - third) * gw
-        tt[3, i] = gx * gy * gw
-        tt[4, i] = gx * gz * gw
-        tt[5, i] = gy * gz * gw
+        tt[2, i] = gx * gy * gw
+        tt[3, i] = gx * gz * gw
+        tt[4, i] = gy * gz * gw
         return carry
 
     lax.fori_loop(0, nzb * count, factor, 0)
@@ -387,6 +408,8 @@
             else:
                 xy = lax.rem(my_zb + r, nzb)
                 remote(src, home, sem_so, sem_ro, (sp, xy * nyb + my_yb)).start()
+
+    def reduce(p, h):
         for g in range(2):
             blocks = pl.ds(g * nyb // 2, nyb // 2)
 
@@ -394,11 +417,11 @@
                 r = i // count
                 o = lax.rem(i, count)
                 prod = mid[p, h, r, o, blocks].astype(F32) * pmid[r, o, p, blocks, h].astype(F32)
-                return tuple(sums[c] + tt[c, i] * prod for c in range(6))
+                return tuple(sums[c] + tt[c, i] * prod for c in range(SENT))
 
             zero = jnp.zeros((nyb // 2, half, nx), F32)
-            sums = lax.fori_loop(0, nzb * count, add_terms, (zero,) * 6)
-            for c in range(6):
+            sums = lax.fori_loop(0, nzb * count, add_terms, (zero,) * SENT)
+            for c in range(SENT):
                 pt[p, h, blocks, c] = sums[c]
         for i in Z_ORDER:
             zc = lax.rem(my_yb + i, nyb)
@@ -414,10 +437,15 @@
 
     def relax(p, h):
         await_copy(rs.at[p, h], sem_rt.at[p, h])
-        for c in range(6):
+        totals = []
+        for c in range(SENT):
             total = rs[p, h, 0, c]
             for s in range(1, nyb):
                 total = total + rs[p, h, s, c]
+            totals.append(total)
+        totals.insert(2, -(totals[0] + totals[1]))
+        for c in range(6):
+            total = totals[c]
             old = wv[c, my_zb * zt + p, pl.ds(pl.multiple_of(my_yb * yt, yt), yt)].astype(F32)
             old = old[h * half : (h + 1) * half]
             value = (1.0 - relax_rate) * old + relax_rate * coupling * total
@@ -443,14 +471,18 @@
     second_step(1, 0)
     second_step(1, 1)
     second_step(0, 0)
-    await_copy(pmid, sem_rp)
     pass_on(1, 0)
     second_step(0, 1)
     pass_on(1, 1)
+    await_copy(pmid, sem_rp)
+    reduce(1, 0)
+    reduce(1, 1)
+    pass_on(0, 0)
+    reduce(0, 0)
     relax(1, 0)
-    pass_on(0, 0)
     relax(1, 1)
     pass_on(0, 1)
+    reduce(0, 1)
     relax(0, 0)
     relax(0, 1)
 
@@ -460,8 +492,7 @@
     drain(nf_hbm, sem_rn)
     drain(out_hbm, sem_ro)
     drain(qext.at[:, pl.ds(0, 2)], sem_hqs)
-    drain(send1.at[0, pl.ds(0, groups - 1)], sem_s1)
-    drain(send1.at[1, pl.ds(0, groups - 1)], sem_s1)
+    drain(send1.at[1, pl.ds(0, groups - 1)], sem_s1.at[nzb])
     drain(pmid.at[pl.ds(0, nzb - 1)], sem_sp)
     drain(ext.at[pl.ds(0, 2), pl.ds(1, yt)], sem_hzs)
     drain(ext.at[0, pl.ds(0, 4)], sem_hys)
@@ -515,9 +546,9 @@
             pltpu.VMEM((nzb, count, ZT, nyb, 2, YT // 2, nx), BF16),
             pltpu.VMEM((ZT, 2, nyb, nzb, count, YT // 2, nx), BF16),
             pltpu.VMEM((ZT, 2, nzb, count, nyb, YT // 2, nx), BF16),
-            pltpu.VMEM((ZT, 2, nyb, 6, YT // 2, nx), F32),
-            pltpu.VMEM((ZT, 2, nyb, 6, YT // 2, nx), F32),
-            pltpu.SMEM((6, nzb * count), F32),
+            pltpu.VMEM((ZT, 2, nyb, SENT, YT // 2, nx), F32),
+            pltpu.VMEM((ZT, 2, nyb, SENT, YT // 2, nx), F32),
+            pltpu.SMEM((SENT, nzb * count), F32),
             pltpu.VMEM((nyb, 6, ZT, pairs, nx), F32),
             pltpu.VMEM((4, no, nx), F32),
             pltpu.VMEM((no, nx), BF16),
@@ -526,7 +557,7 @@
             dma((2,)),
             dma(()),
             dma((ZT,)),
-            dma(()),
+            dma((nzb + 1,)),
             dma(()),
             dma(()),
             dma((2, CHUNKS)),

time: 147 us -> 138 us (0.939)
  Pallas kernels: 144 us -> 135 us
    pallas_call x1, Pallas kernels: 144 us -> 135 us  [per_device(): pl.pallas_call(functools.partial(whole_kernel, dims), in_specs=[hbm] * 6,...]
where the time goes in v5:
time: 138 us
  Pallas kernels  135 us (98%)
  local copies, waits for them, and re-layouts  1.96 us (1%)
    pallas_call x1, Pallas kernels, per_device(): pl.pallas_call(functools.partial(whole_kernel, dims), in_specs=[hbm] * 6,...  135 us

profile of v5, /device:TPU:2, one launch (start us, length us, event | category | flops | bytes accessed | tf_op | source)
XLA Modules:
  0.0 137.5 jit_solution(9195945729707419960)
XLA Ops:
  0.6 134.9 %whole.1 = (bf16[4,16,8,2,8,128]{5,4,3,2,1,0:T(8,128)(2,1)S(1)}, f32[6,16,2,128]{3,2,1,0:T(2,128)S(1)}) custom-call(bf16[4,16,128,128]{3,2,1,0:T(8,128)(2,1)} %q_hbm.1, bf16[4,16,8,2,8,128]{5,4,3,2,1,0:T(8,128)(2,1)} %bitcast.3, bf16[6,16,128,128]{3,2,1,0:T(8,128)(2,1)} %w_hbm.1, bf16[256,256]{1,0:T(8,128)(2,1)} %rot_hbm.1, f32[3,256]{1,0:T(4,128)} %dirs_hbm.1, ...), custom_call_target="tpu_custom_call" | custom-call | tf_op jit(solution)/shard_map/whole/pallas_call | solution.py:526
  135.6 1.3 copy.10
  136.9 0.6 copy.11

commit v6 on v5

--- a/solution.py
+++ b/solution.py
@@ -21,7 +21,7 @@
 EARLY = 0
 WOVEN = 0
 Z_ORDER = (4, 3, 5, 2, 6, 1, 7, 0)
-XY_ORDER = (4, 3, 5, 2, 6, 1, 7, 0)
+XY_ORDER = (0, 1, 7, 2, 6, 3, 5, 4)
 
 
 def whole_kernel(
@@ -413,14 +413,15 @@
         for g in range(2):
             blocks = pl.ds(g * nyb // 2, nyb // 2)
 
-            def add_terms(i, sums, blocks=blocks):
-                r = i // count
-                o = lax.rem(i, count)
-                prod = mid[p, h, r, o, blocks].astype(F32) * pmid[r, o, p, blocks, h].astype(F32)
-                return tuple(sums[c] + tt[c, i] * prod for c in range(SENT))
+            def add_terms(r, sums, blocks=blocks):
+                for o in range(count):
+                    prod = mid[p, h, r, o, blocks].astype(F32)
+                    prod = prod * pmid[r, o, p, blocks, h].astype(F32)
+                    sums = [sums[c] + tt[c, r * count + o] * prod for c in range(SENT)]
+                return tuple(sums)
 
             zero = jnp.zeros((nyb // 2, half, nx), F32)
-            sums = lax.fori_loop(0, nzb * count, add_terms, (zero,) * SENT)
+            sums = lax.fori_loop(0, nzb, add_terms, (zero,) * SENT, unroll=1)
             for c in range(SENT):
                 pt[p, h, blocks, c] = sums[c]
         for i in Z_ORDER:
@@ -471,18 +472,18 @@
     second_step(1, 0)
     second_step(1, 1)
     second_step(0, 0)
+    second_step(0, 1)
     pass_on(1, 0)
-    second_step(0, 1)
-    pass_on(1, 1)
     await_copy(pmid, sem_rp)
     reduce(1, 0)
+    pass_on(1, 1)
     reduce(1, 1)
     pass_on(0, 0)
     reduce(0, 0)
+    pass_on(0, 1)
+    reduce(0, 1)
     relax(1, 0)
     relax(1, 1)
-    pass_on(0, 1)
-    reduce(0, 1)
     relax(0, 0)
     relax(0, 1)
 

time: 138 us -> 137 us (level)
  no operation moved by 1% of the time
where the time goes in v6:
time: 137 us
  Pallas kernels  134 us (98%)
  local copies, waits for them, and re-layouts  1.96 us (1%)
    pallas_call x1, Pallas kernels, per_device(): pl.pallas_call(functools.partial(whole_kernel, dims), in_specs=[hbm] * 6,...  134 us

profile of v6, /device:TPU:2, one launch (start us, length us, event | category | flops | bytes accessed | tf_op | source)
XLA Modules:
  0.0 136.7 jit_solution(7588283841355643056)
XLA Ops:
  0.6 134.1 %whole.1 = (bf16[4,16,8,2,8,128]{5,4,3,2,1,0:T(8,128)(2,1)S(1)}, f32[6,16,2,128]{3,2,1,0:T(2,128)S(1)}) custom-call(bf16[4,16,128,128]{3,2,1,0:T(8,128)(2,1)} %q_hbm.1, bf16[4,16,8,2,8,128]{5,4,3,2,1,0:T(8,128)(2,1)} %bitcast.3, bf16[6,16,128,128]{3,2,1,0:T(8,128)(2,1)} %w_hbm.1, bf16[256,256]{1,0:T(8,128)(2,1)} %rot_hbm.1, f32[3,256]{1,0:T(4,128)} %dirs_hbm.1, ...), custom_call_target="tpu_custom_call" | custom-call | tf_op jit(solution)/shard_map/whole/pallas_call | solution.py:527
  134.7 1.3 copy.10
  136.0 0.6 copy.11

commit v7 on v6

--- a/solution.py
+++ b/solution.py
@@ -20,6 +20,7 @@
 SENT = 5
 EARLY = 0
 WOVEN = 0
+SOON = 6
 Z_ORDER = (4, 3, 5, 2, 6, 1, 7, 0)
 XY_ORDER = (0, 1, 7, 2, 6, 3, 5, 4)
 
@@ -328,7 +329,7 @@
                     y_next,
                 ).start()
 
-    ship_parts(EARLY + WOVEN, (nzb - 1) * zt)
+    ship_parts(EARLY + WOVEN, SOON)
 
     def factor(i, carry):
         o = (lax.rem(my_zb + i // count, nzb) * nyb + my_yb) * count + lax.rem(i, count)
@@ -471,6 +472,7 @@
 
     second_step(1, 0)
     second_step(1, 1)
+    ship_parts(SOON, (nzb - 1) * zt)
     second_step(0, 0)
     second_step(0, 1)
     pass_on(1, 0)

time: 137 us -> 138 us (level)
  no operation moved by 1% of the time
where the time goes in v7:
time: 138 us; the launch traced here: 137 us
  Pallas kernels  135 us (98%)
  local copies, waits for them, and re-layouts  1.96 us (1%)
    pallas_call x1, Pallas kernels, per_device(): pl.pallas_call(functools.partial(whole_kernel, dims), in_specs=[hbm] * 6,...  135 us

profile of v7, /device:TPU:2, one launch (start us, length us, event | category | flops | bytes accessed | tf_op | source)
XLA Modules:
  0.0 137.2 jit_solution(6616693235588941712)
XLA Ops:
  0.6 134.6 %whole.1 = (bf16[4,16,8,2,8,128]{5,4,3,2,1,0:T(8,128)(2,1)S(1)}, f32[6,16,2,128]{3,2,1,0:T(2,128)S(1)}) custom-call(bf16[4,16,128,128]{3,2,1,0:T(8,128)(2,1)} %q_hbm.1, bf16[4,16,8,2,8,128]{5,4,3,2,1,0:T(8,128)(2,1)} %bitcast.3, bf16[6,16,128,128]{3,2,1,0:T(8,128)(2,1)} %w_hbm.1, bf16[256,256]{1,0:T(8,128)(2,1)} %rot_hbm.1, f32[3,256]{1,0:T(4,128)} %dirs_hbm.1, ...), custom_call_target="tpu_custom_call" | custom-call | tf_op jit(solution)/shard_map/whole/pallas_call | solution.py:529
  135.2 1.3 copy.10
  136.5 0.6 copy.11
